TPU v7x, 32 devices: a whole 2x2x4 slice. The times are simulated.
32 devices in a mesh: dp: 4 (over x, core), ctx: 8 (over z, y).
Axes of the slice: x: 2, y: 2, z: 4, core: 2. Of those that a mesh axis runs over, the one named last changes fastest.
Arguments:
- projections: bfloat16 [4, 3, 2048, 1024], P('dp', None, None, 'ctx'), may hold values from -6 to 6
- short_filter: float32 [3, 2048, 3], replicated, may hold values from -3.5 to 3.5
- long_filter: float32 [2048, 1024], P(None, 'ctx'), may hold values from -0.1875 to 0.1875
- skip_gain: float32 [2048], replicated, may hold values from -4 to 4
- cotangent: bfloat16 [4, 2048, 1024], P('dp', None, 'ctx'), may hold values from -6 to 6
Outputs:
- layer_out: bfloat16 [4, 2048, 1024], P('dp', None, 'ctx')
- proj_grad: bfloat16 [4, 3, 2048, 1024], P('dp', None, None, 'ctx')
- filter_grad: float32 [2048, 1024], P('dp', 'ctx')
All inputs are finite; a program needn't handle non-finite values.
Results may differ from a plain program's by a relative error of at most 0.0049.
Values may be sent and summed in bfloat16 or wider, within the bound.
No kernel may reach another device: no remote copies, remote signals or barrier semaphores. Data moves between devices by JAX's collectives and lax.ppermute only.
A program may use at most 128 MiB of HBM per device.

v0:
```python
import math

import jax
import jax.numpy as jnp
from jax import lax
from jax.sharding import PartitionSpec as P

exact_mode = lax.Precision.HIGHEST


def passed_along(block, axis, distance):
    devices = range(lax.axis_size(axis))
    route = [(i - distance, i) for i in devices if i - distance in devices]
    return lax.ppermute(block, axis, route)


def angle_table(rows, cols, period):
    row_index = lax.broadcasted_iota(jnp.int32, (rows, cols), 0)
    col_index = lax.broadcasted_iota(jnp.int32, (rows, cols), 1)
    product = row_index * col_index % period
    return product.astype(jnp.float32) * (2.0 * math.pi / period)


def forward_dft(signal):
    groups = signal.shape[0]
    blocks = signal.shape[1]
    inner = signal.shape[3]
    outer = 2 * blocks
    total = outer * inner
    first_angle = angle_table(outer, blocks, outer)
    first_cos = jnp.broadcast_to(jnp.cos(first_angle), (groups, outer, blocks))
    first_sin = jnp.broadcast_to(-jnp.sin(first_angle), (groups, outer, blocks))
    part_real = jnp.einsum("dqp,dpsr->dqsr", first_cos, signal, precision=exact_mode)
    part_imag = jnp.einsum("dqp,dpsr->dqsr", first_sin, signal, precision=exact_mode)
    twist = angle_table(outer, inner, total)
    twist_cos = jnp.cos(twist)[None, :, None, :]
    twist_sin = jnp.sin(twist)[None, :, None, :]
    mid_real = part_real * twist_cos + part_imag * twist_sin
    mid_imag = part_imag * twist_cos - part_real * twist_sin
    last_angle = angle_table(inner, inner, inner)
    last_cos = jnp.cos(last_angle)
    last_sin = jnp.sin(last_angle)
    out_real = jnp.einsum("dqsr,rm->dqsm", mid_real, last_cos, precision=exact_mode) + jnp.einsum(
        "dqsr,rm->dqsm", mid_imag, last_sin, precision=exact_mode
    )
    out_imag = jnp.einsum("dqsr,rm->dqsm", mid_imag, last_cos, precision=exact_mode) - jnp.einsum(
        "dqsr,rm->dqsm", mid_real, last_sin, precision=exact_mode
    )
    return (out_real, out_imag)


def inverse_dft(spectrum):
    spec_real, spec_imag = spectrum
    groups = spec_real.shape[0]
    outer = spec_real.shape[1]
    inner = spec_real.shape[3]
    blocks = outer // 2
    total = outer * inner
    last_angle = angle_table(inner, inner, inner)
    last_cos = jnp.cos(last_angle)
    last_sin = jnp.sin(last_angle)
    mid_real = jnp.einsum("dqsm,mr->dqsr", spec_real, last_cos, precision=exact_mode) - jnp.einsum(
        "dqsm,mr->dqsr", spec_imag, last_sin, precision=exact_mode
    )
    mid_imag = jnp.einsum("dqsm,mr->dqsr", spec_real, last_sin, precision=exact_mode) + jnp.einsum(
        "dqsm,mr->dqsr", spec_imag, last_cos, precision=exact_mode
    )
    twist = angle_table(outer, inner, total)
    twist_cos = jnp.cos(twist)[None, :, None, :]
    twist_sin = jnp.sin(twist)[None, :, None, :]
    turned_real = mid_real * twist_cos - mid_imag * twist_sin
    turned_imag = mid_real * twist_sin + mid_imag * twist_cos
    first_angle = angle_table(blocks, outer, outer)
    first_cos = jnp.broadcast_to(jnp.cos(first_angle), (groups, blocks, outer))
    first_sin = jnp.broadcast_to(jnp.sin(first_angle), (groups, blocks, outer))
    result = jnp.einsum(
        "dpq,dqsr->dpsr", first_cos, turned_real, precision=exact_mode
    ) - jnp.einsum("dpq,dqsr->dpsr", first_sin, turned_imag, precision=exact_mode)
    return result * (1.0 / total)


def spec_product(left, right):
    return (left[0] * right[0] - left[1] * right[1], left[0] * right[1] + left[1] * right[0])


def conj_product(left, right):
    return (left[0] * right[0] + left[1] * right[1], left[0] * right[1] - left[1] * right[0])


def shards(projections, short_filter, long_filter, skip_gain, cotangent):
    dp_count = lax.axis_size("dp")
    ctx_count = lax.axis_size("ctx")
    channels = projections.shape[2]
    inner = projections.shape[3]
    slab = channels // (dp_count * ctx_count)
    length = inner * ctx_count
    tap_zero = short_filter[:, :, 0:1]
    tap_one = short_filter[:, :, 1:2]
    tap_two = short_filter[:, :, 2:3]
    skip_col = skip_gain[:, None]
    local_proj = projections[0]
    edge = passed_along(local_proj[:, :, inner - 2 :], "ctx", 1)
    extended = jnp.concatenate([edge, local_proj], axis=2).astype(jnp.float32)
    act = (
        tap_zero * extended[:, :, 2:]
        + tap_one * extended[:, :, 1 : inner + 1]
        + tap_two * extended[:, :, 0:inner]
    )
    first = act[0]
    second = act[1]
    value = act[2]
    gate = (first * value).astype(jnp.bfloat16)
    upstream = cotangent[0].astype(jnp.float32)
    grad = (upstream * second).astype(jnp.bfloat16)
    gate_rows = gate.reshape(dp_count, ctx_count, slab, inner)
    grad_rows = grad.reshape(dp_count, ctx_count, slab, inner)
    gate_ch = lax.all_to_all(gate_rows, "ctx", split_axis=1, concat_axis=1, tiled=True)
    grad_ch = lax.all_to_all(grad_rows, "ctx", split_axis=1, concat_axis=1, tiled=True)
    filter_ch = lax.all_to_all(
        long_filter.reshape(dp_count, ctx_count, slab, inner),
        "ctx",
        split_axis=1,
        concat_axis=1,
        tiled=True,
    )
    filter_spec = forward_dft(filter_ch)
    gate_spec = forward_dft(gate_ch.astype(jnp.float32))
    grad_spec = forward_dft(grad_ch.astype(jnp.float32))
    conv_ch = inverse_dft(spec_product(filter_spec, gate_spec))
    corr_ch = inverse_dft(conj_product(filter_spec, grad_spec))
    fgrad_ch = inverse_dft(conj_product(gate_spec, grad_spec))
    fgrad_send = lax.psum_scatter(fgrad_ch, "dp", scatter_dimension=0, tiled=True)
    conv_pos = lax.all_to_all(conv_ch, "ctx", split_axis=1, concat_axis=1, tiled=True)
    corr_pos, fgrad_back = (
        lax.all_to_all(corr_ch, "ctx", split_axis=1, concat_axis=1, tiled=True),
        lax.all_to_all(fgrad_send, "ctx", split_axis=1, concat_axis=1, tiled=True),
    )
    filter_grad = fgrad_back.reshape(channels // dp_count, inner) * (
        1.0 / math.sqrt(dp_count * length)
    )
    conv = conv_pos.reshape(channels, inner)
    mixed = conv + skip_col * gate.astype(jnp.float32)
    layer_out = (second * mixed).astype(jnp.bfloat16)
    gate_grad = corr_pos.reshape(channels, inner) + skip_col * grad.astype(jnp.float32)
    act_grad = jnp.stack([gate_grad * value, upstream * mixed, gate_grad * first])
    tail = passed_along(act_grad[:, :, 0:2], "ctx", -1)
    widened = jnp.concatenate([act_grad, tail], axis=2)
    proj_back = (
        tap_zero * widened[:, :, 0:inner]
        + tap_one * widened[:, :, 1 : inner + 1]
        + tap_two * widened[:, :, 2 : inner + 2]
    )
    return (layer_out[None], proj_back.astype(jnp.bfloat16)[None], filter_grad)


def solution(mesh):
    placed = (P("dp", None, None, "ctx"), P(), P(None, "ctx"), P(), P("dp", None, "ctx"))
    return jax.shard_map(
        shards,
        mesh=mesh,
        in_specs=placed,
        out_specs=(P("dp", None, "ctx"), P("dp", None, None, "ctx"), P("dp", "ctx")),
        check_vma=False,
    )
```

profile of v0, /device:TPU:0, one launch (start us, length us, event | category | flops | bytes accessed | tf_op | source)
XLA Modules:
  0.0 263.6 jit_solution(6697983948489987695)
XLA Ops:
  7.2 1.9 slice.52
  9.8 4.9 %collective-permute-start = (bf16[3,2048,2]{1,2,0:T(2,128)(2,1)S(1)}, bf16[3,2048,2]{1,2,0:T(2,128)(2,1)S(1)}, u32[]{:S(2)}, u32[]{:S(2)}) collective-permute-start(bf16[3,2048,2]{1,2,0:T(2,128)(2,1)S(1)} %copy.62), channel_id=1, source_target_pairs={{0,1},{1,2},{2,3},{3,4},{4,5},{5,6},{6,7},{8,9},{9,10},{10,11},{11... | collective-permute-start | bytes 73736 | tf_op jit(solution)/shard_map/ppermute | solution.py:14
  14.9 1.4 collective-permute-done
  18.3 4.7 %fusion.3 = f32[3,2048,128]{2,1,0:T(8,128)S(1)} fusion(f32[3,2048,130]{2,1,0:T(8,128)S(1)} %maximum_convert_fusion, f32[3,2048]{1,0:T(4,128)S(1)} %get-tuple-element.32, f32[3,2048]{1,0:T(4,128)S(1)} %get-tuple-element.33, f32[3,2048]{1,0:T(4,128)S(1)} %bitcast.113), kind=kLoop, calls=%fused_computation.7 | loop fusion | flops 3932160 | bytes 12656640 | tf_op jit(solution)/shard_map/add | solution.py:105
  25.6 6.6 %all-to-all-start.3 = ((bf16[4,8,64,128]{3,2,0,1:T(8,128)(2,1)}), bf16[4,8,64,128]{3,2,0,1:T(8,128)(2,1)}, u32[]{:S(2)}, u32[]{:S(2)}) async-start(bf16[4,8,64,128]{3,2,0,1:T(8,128)(2,1)} %copy.84), calls=%async_computation.3 | async-start | bytes 1048576 | tf_op jit(solution)/shard_map/all_to_all | solution.py:118
  32.2 1.9 copy.69
  34.2 11.5 %all-to-all-done.3 = bf16[4,8,64,128]{3,2,0,1:T(8,128)(2,1)} async-done(((bf16[4,8,64,128]{3,2,0,1:T(8,128)(2,1)}), bf16[4,8,64,128]{3,2,0,1:T(8,128)(2,1)}, u32[]{:S(2)}, u32[]{:S(2)}) %all-to-all-start.3) | async-done | bytes 524320 | tf_op jit(solution)/shard_map/all_to_all | solution.py:118
  45.7 4.2 %all-to-all-start.1 = ((bf16[4,8,64,128]{3,2,0,1:T(8,128)(2,1)}), bf16[4,8,64,128]{3,2,0,1:T(8,128)(2,1)}, u32[]{:S(2)}, u32[]{:S(2)}) async-start(bf16[4,8,64,128]{3,2,0,1:T(8,128)(2,1)} %copy.69), calls=%async_computation.1 | async-start | bytes 1048576 | tf_op jit(solution)/shard_map/all_to_all | solution.py:117
  49.9 2.3 copy.64
  52.2 11.1 %all-to-all-done.1 = bf16[4,8,64,128]{3,2,0,1:T(8,128)(2,1)} async-done(((bf16[4,8,64,128]{3,2,0,1:T(8,128)(2,1)}), bf16[4,8,64,128]{3,2,0,1:T(8,128)(2,1)}, u32[]{:S(2)}, u32[]{:S(2)}) %all-to-all-start.1) | async-done | bytes 524320 | tf_op jit(solution)/shard_map/all_to_all | solution.py:117
  63.2 4.4 %all-to-all-start = ((f32[4,8,64,128]{3,2,0,1:T(8,128)}), f32[4,8,64,128]{3,2,0,1:T(8,128)}, u32[]{:S(2)}, u32[]{:S(2)}) async-start(f32[4,8,64,128]{3,2,0,1:T(8,128)} %copy.64), calls=%async_computation | async-start | bytes 2097152 | tf_op jit(solution)/shard_map/all_to_all | solution.py:119
  67.9 3.5 %fusion.151 = f32[4,16,64,128]{3,1,2,0:T(8,128)} fusion(bf16[4,8,64,128]{3,2,0,1:T(8,128)(2,1)} %all-to-all-done.3, f32[16,8]{0,1:T(8,128)S(1)} %fusion.257), kind=kOutput, calls=%fused_computation.143 | convolution fusion | flops 50331648 | bytes 2621952 | tf_op jit(solution)/shard_map/dqp,dpsr->dqsr/dot_general | solution.py:33
  71.4 3.4 %fusion.155 = f32[4,16,64,128]{3,1,2,0:T(8,128)} fusion(bf16[4,8,64,128]{3,2,0,1:T(8,128)(2,1)} %all-to-all-done.1, f32[16,8]{0,1:T(8,128)S(1)} %fusion.257), kind=kOutput, calls=%fused_computation.147 | convolution fusion | flops 50331648 | bytes 2621952 | tf_op jit(solution)/shard_map/dqp,dpsr->dqsr/dot_general | solution.py:33
  74.8 3.5 %fusion.153 = f32[4,16,64,128]{3,1,2,0:T(8,128)} fusion(bf16[4,8,64,128]{3,2,0,1:T(8,128)(2,1)} %all-to-all-done.1, f32[16,8]{0,1:T(8,128)S(1)} %sine_negate_fusion), kind=kOutput, calls=%fused_computation.145 | convolution fusion | flops 50331648 | bytes 2621952 | tf_op jit(solution)/shard_map/dqp,dpsr->dqsr/dot_general | solution.py:34
  78.3 14.0 %all-to-all-done = f32[4,8,64,128]{3,2,0,1:T(8,128)} async-done(((f32[4,8,64,128]{3,2,0,1:T(8,128)}), f32[4,8,64,128]{3,2,0,1:T(8,128)}, u32[]{:S(2)}, u32[]{:S(2)}) %all-to-all-start) | async-done | bytes 1048608 | tf_op jit(solution)/shard_map/all_to_all | solution.py:119
  92.3 3.6 %fusion.145 = f32[4,16,64,128]{3,1,2,0:T(8,128)S(1)} fusion(f32[4,8,64,128]{3,2,0,1:T(8,128)} %all-to-all-done, f32[16,8]{0,1:T(8,128)S(1)} %sine_negate_fusion), kind=kOutput, calls=%fused_computation.137 | convolution fusion | flops 50331648 | bytes 3146240 | tf_op jit(solution)/shard_map/dqp,dpsr->dqsr/dot_general | solution.py:34
  95.8 3.6 %fusion.147 = f32[4,16,64,128]{3,1,2,0:T(8,128)S(1)} fusion(f32[4,8,64,128]{3,2,0,1:T(8,128)} %all-to-all-done, f32[16,8]{0,1:T(8,128)S(1)} %fusion.257), kind=kOutput, calls=%fused_computation.139 | convolution fusion | flops 50331648 | bytes 3146240 | tf_op jit(solution)/shard_map/dqp,dpsr->dqsr/dot_general | solution.py:33
  99.4 3.3 %multiply_add_fusion.2 = (f32[4,16,64,128]{3,1,2,0:T(8,128)S(1)}, f32[4,16,64,128]{3,1,2,0:T(8,128)S(1)}, f32[4,16,64,128]{3,1,2,0:T(8,128)S(1)}, f32[4,16,64,12...) fusion(f32[4,16,64,128]{3,1,2,0:T(8,128)S(1)} %copy-done.12, ...), kind=kOutput, calls=%fused_computation.34 | convolution fusion | flops 59768832 | bytes 23609856 | tf_op jit(solution)/shard_map/dqp,dpsr->dqsr/dot_general | solution.py:34
  102.7 2.8 %fusion.71 = f32[4,16,64,128]{3,2,1,0:T(8,128)S(1)} fusion(f32[4,16,64,128]{3,1,2,0:T(8,128)S(1)} %get-tuple-element.30), kind=kOutput, calls=%fused_computation.91 | convolution fusion | flops 805535744 | bytes 4194304 | tf_op jit(solution)/shard_map/dqsr,rm->dqsm/dot_general | solution.py:43
  105.5 2.5 fusion.69
  108.0 2.5 fusion.55
  110.5 2.5 fusion.53
  113.0 2.5 fusion.63
  115.5 2.9 %fusion.61 = f32[4,16,64,128]{3,2,1,0:T(8,128)S(1)} fusion(f32[4,16,64,128]{3,1,2,0:T(8,128)S(1)} %get-tuple-element.28), kind=kOutput, calls=%fused_computation.81 | convolution fusion | flops 805535744 | bytes 4194304 | tf_op jit(solution)/shard_map/dqsr,rm->dqsm/dot_general | solution.py:46
  118.4 2.5 fusion.77
  120.9 2.5 fusion.80
  123.5 2.5 fusion.89
  126.0 2.5 fusion.92
  128.5 2.7 %fusion.83 = f32[4,16,64,128]{3,2,1,0:T(8,128)S(1)} fusion(f32[4,16,64,128]{3,2,1,0:T(8,128)S(1)} %fusion.63, f32[4,16,64,128]{3,1,2,0:T(8,128)S(1)} %get-tuple-element.29), kind=kOutput, calls=%fused_computation.99 | convolution fusion | flops 806060032 | bytes 6291456 | tf_op jit(solution)/shard_map/dqsr,rm->dqsm/dot_general | solution.py:43
  131.2 5.3 %multiply_add_fusion = (f32[4,16,64,128]{3,2,1,0:T(8,128)}, f32[4,16,64,128]{3,2,1,0:T(8,128)}, f32[4,16,64,128]{3,2,1,0:T(8,128)S(1)}, f32[4,16,64,128]{3,2,1,0...) fusion(f32[4,16,64,128]{3,2,1,0:T(8,128)S(1)} %fusion.92, f32[4,16,64,128]{3,2,1,0:T(8,128)S(1)} %fusion.83, ...), kind=kOutput, calls=%fused_computation.22 | convolution fusion | flops 815497216 | bytes 27262976 | tf_op jit(solution)/shard_map/dqsr,rm->dqsm/dot_general | solution.py:46
  136.5 3.2 %fusion.47 = f32[4,16,64,128]{3,1,2,0:T(8,128)S(1)} fusion(f32[4,16,64,128]{3,2,1,0:T(8,128)S(1)} %get-tuple-element.19), kind=kOutput, calls=%fused_computation.67 | convolution fusion | flops 805535744 | bytes 4194304 | tf_op jit(solution)/shard_map/dqsm,mr->dqsr/dot_general | solution.py:62
  139.6 3.2 %fusion.45 = f32[4,16,64,128]{3,1,2,0:T(8,128)S(1)} fusion(f32[4,16,64,128]{3,2,1,0:T(8,128)S(1)} %get-tuple-element.19), kind=kOutput, calls=%fused_computation.65 | convolution fusion | flops 805535744 | bytes 4194304 | tf_op jit(solution)/shard_map/dqsm,mr->dqsr/dot_general | solution.py:65
  142.8 4.4 %fusion.39 = f32[4,16,64,128]{3,1,2,0:T(8,128)} fusion(f32[4,16,64,128]{3,2,1,0:T(8,128)S(1)} %get-tuple-element.17), kind=kOutput, calls=%fused_computation.59 | convolution fusion | flops 805535744 | bytes 4194304 | tf_op jit(solution)/shard_map/dqsm,mr->dqsr/dot_general | solution.py:62
  147.3 4.9 %fusion.37 = f32[4,16,64,128]{3,1,2,0:T(8,128)} fusion(f32[4,16,64,128]{3,2,1,0:T(8,128)S(1)} %get-tuple-element.17), kind=kOutput, calls=%fused_computation.57 | convolution fusion | flops 805535744 | bytes 4194304 | tf_op jit(solution)/shard_map/dqsm,mr->dqsr/dot_general | solution.py:65
  152.2 3.2 %fusion.95 = f32[4,16,64,128]{3,1,2,0:T(8,128)S(1)} fusion(f32[4,16,64,128]{3,1,2,0:T(8,128)S(1)} %fusion.47, f32[4,16,64,128]{3,2,1,0:T(8,128)S(1)} %get-tuple-element.20), kind=kOutput, calls=%fused_computation.103 | convolution fusion | flops 806060032 | bytes 6291456 | tf_op jit(solution)/shard_map/dqsm,mr->dqsr/dot_general | solution.py:62
  155.4 3.2 %fusion.98 = f32[4,16,64,128]{3,1,2,0:T(8,128)S(1)} fusion(f32[4,16,64,128]{3,1,2,0:T(8,128)S(1)} %fusion.45, f32[4,16,64,128]{3,2,1,0:T(8,128)S(1)} %get-tuple-element.20), kind=kOutput, calls=%fused_computation.104 | convolution fusion | flops 806060032 | bytes 6291456 | tf_op jit(solution)/shard_map/dqsm,mr->dqsr/dot_general | solution.py:65
  158.6 1.3 fusion.21
  159.9 1.4 fusion.129
  161.3 1.2 copy.82
  162.5 4.4 %all-to-all-start.2 = ((f32[4,8,64,128]{3,2,0,1:T(8,128)}), f32[4,8,64,128]{3,2,0,1:T(8,128)}, u32[]{:S(2)}, u32[]{:S(2)}) async-start(f32[4,8,64,128]{3,2,0,1:T(8,128)} %copy.82), calls=%async_computation.2 | async-start | bytes 2097152 | tf_op jit(solution)/shard_map/all_to_all | solution.py:133
  166.9 5.4 %fusion.101 = f32[4,16,64,128]{3,1,2,0:T(8,128)S(1)} fusion(f32[4,16,64,128]{3,1,2,0:T(8,128)} %fusion.39, f32[4,16,64,128]{3,2,1,0:T(8,128)} %get-tuple-element.18), kind=kOutput, calls=%fused_computation.105 | convolution fusion | flops 806060032 | bytes 6291456 | tf_op jit(solution)/shard_map/dqsm,mr->dqsr/dot_general | solution.py:62
  172.4 3.2 %fusion.104 = f32[4,16,64,128]{3,1,2,0:T(8,128)S(1)} fusion(f32[4,16,64,128]{3,1,2,0:T(8,128)S(1)} %copy-done.11, f32[4,16,64,128]{3,2,1,0:T(8,128)S(1)} %copy-done.3), kind=kOutput, calls=%fused_computation.106 | convolution fusion | flops 806060032 | bytes 6291456 | tf_op jit(solution)/shard_map/dqsm,mr->dqsr/dot_general | solution.py:65
  175.6 1.3 fusion.13
  176.9 1.4 fusion.126
  180.3 3.2 %fusion.31 = f32[4,16,64,128]{3,1,2,0:T(8,128)S(1)} fusion(f32[4,16,64,128]{3,2,1,0:T(8,128)S(1)} %copy-done.4), kind=kOutput, calls=%fused_computation.51 | convolution fusion | flops 805535744 | bytes 4194304 | tf_op jit(solution)/shard_map/dqsm,mr->dqsr/dot_general | solution.py:62
  183.4 4.6 %fusion.107 = f32[4,16,64,128]{3,1,2,0:T(8,128)} fusion(f32[4,16,64,128]{3,1,2,0:T(8,128)S(1)} %fusion.31, f32[4,16,64,128]{3,2,1,0:T(8,128)S(1)} %copy-done.1), kind=kOutput, calls=%fused_computation.107 | convolution fusion | flops 806060032 | bytes 6291456 | tf_op jit(solution)/shard_map/dqsm,mr->dqsr/dot_general | solution.py:62
  188.0 4.2 %all-to-all-done.2 = f32[4,8,64,128]{3,2,0,1:T(8,128)} async-done(((f32[4,8,64,128]{3,2,0,1:T(8,128)}), f32[4,8,64,128]{3,2,0,1:T(8,128)}, u32[]{:S(2)}, u32[]{:S(2)}) %all-to-all-start.2) | async-done | bytes 1048608 | tf_op jit(solution)/shard_map/all_to_all | solution.py:133
  192.2 4.2 %all-to-all-start.4 = ((f32[4,8,64,128]{3,2,0,1:T(8,128)}), f32[4,8,64,128]{3,2,0,1:T(8,128)}, u32[]{:S(2)}, u32[]{:S(2)}) async-start(f32[4,8,64,128]{3,2,0,1:T(8,128)} %copy.95), calls=%async_computation.4 | async-start | bytes 2097152 | tf_op jit(solution)/shard_map/all_to_all | solution.py:135
  196.7 4.7 %fusion.29 = f32[4,16,64,128]{3,1,2,0:T(8,128)S(1)} fusion(f32[4,16,64,128]{3,2,1,0:T(8,128)} %get-tuple-element.4), kind=kOutput, calls=%fused_computation.49 | convolution fusion | flops 805535744 | bytes 4194304 | tf_op jit(solution)/shard_map/dqsm,mr->dqsr/dot_general | solution.py:65
  201.5 3.2 %fusion.110 = f32[4,16,64,128]{3,1,2,0:T(8,128)S(1)} fusion(f32[4,16,64,128]{3,1,2,0:T(8,128)S(1)} %fusion.29, f32[4,16,64,128]{3,2,1,0:T(8,128)S(1)} %copy-done.2), kind=kOutput, calls=%fused_computation.108 | convolution fusion | flops 806060032 | bytes 6291456 | tf_op jit(solution)/shard_map/dqsm,mr->dqsr/dot_general | solution.py:65
  204.7 1.3 fusion.5
  206.1 2.3 fusion.123
  208.4 2.4 copy.83
  210.8 11.0 %all-to-all-done.4 = f32[4,8,64,128]{3,2,0,1:T(8,128)} async-done(((f32[4,8,64,128]{3,2,0,1:T(8,128)}), f32[4,8,64,128]{3,2,0,1:T(8,128)}, u32[]{:S(2)}, u32[]{:S(2)}) %all-to-all-start.4) | async-done | bytes 1048608 | tf_op jit(solution)/shard_map/all_to_all | solution.py:135
  221.8 1.5 copy.96
  223.7 2.4 slice_multiply_fusion.5
  227.8 1.2 copy.97
  229.0 1.6 collective-permute-start.1
  230.5 4.7 %collective-permute-done.1 = f32[3,2048,2]{1,2,0:T(2,128)S(1)} collective-permute-done((f32[3,2048,2]{1,2,0:T(2,128)S(1)}, f32[3,2048,2]{1,2,0:T(2,128)S(1)}, u32[]{:S(2)}, u32[]{:S(2)}) %collective-permute-start.1) | collective-permute-done | bytes 49184 | tf_op jit(solution)/shard_map/ppermute | solution.py:14
  235.2 2.2 copy.98
  237.4 4.3 %pad_maximum_fusion = f32[3,2048,130]{2,1,0:T(8,128)} fusion(f32[3,2048,2]{2,1,0:T(8,128)} %copy.98, f32[1,2048,128]{2,1,0:T(8,128)S(1)} %copy-done.8, f32[1,2048,128]{2,1,0:T(8,128)S(1)} %copy-done.10, f32[1,2048,128]{2,1,0:T(8,128)S(1)} %copy-done.6), kind=kLoop, calls=%fused_computation | loop fusion | flops 2396160 | bytes 6389760 | tf_op jit(solution)/shard_map/concatenate | solution.py:147
  241.7 1.7 copy.103
  243.4 3.4 %all-to-all-start.5 = ((f32[1,8,64,128]{3,2,0,1:T(8,128)}), f32[1,8,64,128]{3,2,0,1:T(8,128)S(1)}, u32[]{:S(2)}, u32[]{:S(2)}) async-start(f32[1,8,64,128]{3,2,0,1:T(8,128)} %copy.103), calls=%async_computation.6 | async-start | bytes 524288 | tf_op jit(solution)/shard_map/all_to_all | solution.py:136
  246.8 8.9 %fusion.113 = bf16[1,3,2048,128]{3,2,1,0:T(8,128)(2,1)} fusion(f32[3,2048,130]{2,1,0:T(8,128)} %pad_maximum_fusion, f32[3,2048]{1,0:T(4,128)S(1)} %get-tuple-element.32, f32[3,2048]{1,0:T(4,128)S(1)} %get-tuple-element.33, f32[3,2048]{1,0:T(4,128)S(1)} %bitcast.114, f32[1,2048,128]{2,1,0:T(8,128)S(1)} %copy-done.8, f32[1,2048,128]{2,1,0:T(8,128)S(1)} %copy-done.10, ...), kind=kLoop, calls=%fused_computation.109 | loop fusion | flops 6291456 | bytes 11083776 | tf_op jit(solution)/shard_map/broadcast_in_dim | solution.py:153
  (66 shorter events, 10.8 us)
Async XLA Ops:
  7.2 7.6 %copy-start.21 = (f32[3,2048,3]{1,2,0:T(4,128)S(1)}, f32[3,2048,3]{1,2,0:T(4,128)}, u32[]{:S(2)}) copy-start(f32[3,2048,3]{1,2,0:T(4,128)} %param.6) | copy-start | bytes 221188
  9.1 8.0 %copy-start.15 = (bf16[1,3,2048,128]{3,2,1,0:T(8,128)(2,1)S(1)}, bf16[1,3,2048,128]{3,2,1,0:T(8,128)(2,1)}, u32[]{:S(2)}) copy-start(bf16[1,3,2048,128]{3,2,1,0:T(8,128)(2,1)} %param.5) | copy-start | bytes 4718596
  9.8 6.4 %collective-permute-start = (bf16[3,2048,2]{1,2,0:T(2,128)(2,1)S(1)}, bf16[3,2048,2]{1,2,0:T(2,128)(2,1)S(1)}, u32[]{:S(2)}, u32[]{:S(2)}) collective-permute-start(bf16[3,2048,2]{1,2,0:T(2,128)(2,1)S(1)} %copy.62), channel_id=1, source_target_pairs={{0,1},{1,2},{2,3},{3,4},{4,5},{5,6},{6,7},{8,9},{9,10},{10,11},{11... | collective-permute-start | bytes 73736 | tf_op jit(solution)/shard_map/ppermute | solution.py:14
  18.3 4.7 %copy-start.20 = (bf16[1,2048,128]{2,1,0:T(8,128)(2,1)S(1)}, bf16[1,2048,128]{2,1,0:T(8,128)(2,1)}, u32[]{:S(2)}) copy-start(bf16[1,2048,128]{2,1,0:T(8,128)(2,1)} %param.9) | copy-start | bytes 1572868
  24.0 0.8 copy-start.16
  25.6 20.1 %all-to-all-start.3 = ((bf16[4,8,64,128]{3,2,0,1:T(8,128)(2,1)}), bf16[4,8,64,128]{3,2,0,1:T(8,128)(2,1)}, u32[]{:S(2)}, u32[]{:S(2)}) async-start(bf16[4,8,64,128]{3,2,0,1:T(8,128)(2,1)} %copy.84), calls=%async_computation.3 | async-start | bytes 1048576 | tf_op jit(solution)/shard_map/all_to_all | solution.py:118
  45.7 17.5 %all-to-all-start.1 = ((bf16[4,8,64,128]{3,2,0,1:T(8,128)(2,1)}), bf16[4,8,64,128]{3,2,0,1:T(8,128)(2,1)}, u32[]{:S(2)}, u32[]{:S(2)}) async-start(bf16[4,8,64,128]{3,2,0,1:T(8,128)(2,1)} %copy.69), calls=%async_computation.1 | async-start | bytes 1048576 | tf_op jit(solution)/shard_map/all_to_all | solution.py:117
  63.2 29.0 %all-to-all-start = ((f32[4,8,64,128]{3,2,0,1:T(8,128)}), f32[4,8,64,128]{3,2,0,1:T(8,128)}, u32[]{:S(2)}, u32[]{:S(2)}) async-start(f32[4,8,64,128]{3,2,0,1:T(8,128)} %copy.64), calls=%async_computation | async-start | bytes 2097152 | tf_op jit(solution)/shard_map/all_to_all | solution.py:119
  92.2 7.1 %copy-start.13 = (f32[4,16,64,128]{3,1,2,0:T(8,128)S(1)}, f32[4,16,64,128]{3,1,2,0:T(8,128)}, u32[]{:S(2)}) copy-start(f32[4,16,64,128]{3,1,2,0:T(8,128)} %fusion.155) | copy-start | bytes 6291460
  92.2 7.1 %copy-start.14 = (f32[4,16,64,128]{3,1,2,0:T(8,128)S(1)}, f32[4,16,64,128]{3,1,2,0:T(8,128)}, u32[]{:S(2)}) copy-start(f32[4,16,64,128]{3,1,2,0:T(8,128)} %fusion.153) | copy-start | bytes 6291460
  95.8 3.6 %copy-start.12 = (f32[4,16,64,128]{3,1,2,0:T(8,128)S(1)}, f32[4,16,64,128]{3,1,2,0:T(8,128)}, u32[]{:S(2)}) copy-start(f32[4,16,64,128]{3,1,2,0:T(8,128)} %fusion.151) | copy-start | bytes 6291460
  162.5 29.7 %all-to-all-start.2 = ((f32[4,8,64,128]{3,2,0,1:T(8,128)}), f32[4,8,64,128]{3,2,0,1:T(8,128)}, u32[]{:S(2)}, u32[]{:S(2)}) async-start(f32[4,8,64,128]{3,2,0,1:T(8,128)} %copy.82), calls=%async_computation.2 | async-start | bytes 2097152 | tf_op jit(solution)/shard_map/all_to_all | solution.py:133
  166.9 5.4 %copy-start.3 = (f32[4,16,64,128]{3,2,1,0:T(8,128)S(1)}, f32[4,16,64,128]{3,2,1,0:T(8,128)}, u32[]{:S(2)}) copy-start(f32[4,16,64,128]{3,2,1,0:T(8,128)} %get-tuple-element.18) | copy-start | bytes 6291460
  166.9 5.4 %copy-start.11 = (f32[4,16,64,128]{3,1,2,0:T(8,128)S(1)}, f32[4,16,64,128]{3,1,2,0:T(8,128)}, u32[]{:S(2)}) copy-start(f32[4,16,64,128]{3,1,2,0:T(8,128)} %fusion.37) | copy-start | bytes 6291460
  178.3 2.0 copy-start.4
  180.3 3.2 %copy-start.1 = (f32[4,16,64,128]{3,2,1,0:T(8,128)S(1)}, f32[4,16,64,128]{3,2,1,0:T(8,128)}, u32[]{:S(2)}) copy-start(f32[4,16,64,128]{3,2,1,0:T(8,128)} %get-tuple-element.3) | copy-start | bytes 6291460
  192.2 29.6 %all-to-all-start.4 = ((f32[4,8,64,128]{3,2,0,1:T(8,128)}), f32[4,8,64,128]{3,2,0,1:T(8,128)}, u32[]{:S(2)}, u32[]{:S(2)}) async-start(f32[4,8,64,128]{3,2,0,1:T(8,128)} %copy.95), calls=%async_computation.4 | async-start | bytes 2097152 | tf_op jit(solution)/shard_map/all_to_all | solution.py:135
  196.4 45.3 %reduce-scatter.2.cloned.1.call-start = ((), (), s32[]{:S(2)}) async-start(), calls=%async_computation.7 | async-start | bytes 1310720 | tf_op jit(solution)/shard_map/reduce_scatter | solution.py:132
  196.7 4.8 %copy-start.2 = (f32[4,16,64,128]{3,2,1,0:T(8,128)S(1)}, f32[4,16,64,128]{3,2,1,0:T(8,128)}, u32[]{:S(2)}) copy-start(f32[4,16,64,128]{3,2,1,0:T(8,128)} %get-tuple-element.3) | copy-start | bytes 6291460
  201.5 3.2 %copy-start = (f32[4,16,64,128]{3,1,2,0:T(8,128)S(1)}, f32[4,16,64,128]{3,1,2,0:T(8,128)}, u32[]{:S(2)}) copy-start(f32[4,16,64,128]{3,1,2,0:T(8,128)} %fusion.107) | copy-start | bytes 6291460
  208.4 14.9 %copy-start.22 = (f32[2048]{0:T(1024)S(1)}, f32[2048]{0:T(1024)}, u32[]{:S(2)}) copy-start(f32[2048]{0:T(1024)} %param.8) | copy-start | bytes 24580
  221.8 1.5 copy-start.17
  221.8 1.5 copy-start.18
  221.8 1.9 copy-start.19
  226.1 1.0 copy-start.5
  226.1 1.3 copy-start.7
  226.1 1.7 copy-start.9
  228.9 8.5 %copy-start.6 = (f32[1,2048,128]{2,1,0:T(8,128)S(1)}, f32[1,2048,128]{2,1,0:T(8,128)}, u32[]{:S(2)}) copy-start(f32[1,2048,128]{2,1,0:T(8,128)} %copy-done.5) | copy-start | bytes 3145732
  228.9 8.5 %copy-start.8 = (f32[1,2048,128]{2,1,0:T(8,128)S(1)}, f32[1,2048,128]{2,1,0:T(8,128)}, u32[]{:S(2)}) copy-start(f32[1,2048,128]{2,1,0:T(8,128)} %copy-done.7) | copy-start | bytes 3145732
  229.0 8.5 %copy-start.10 = (f32[1,2048,128]{2,1,0:T(8,128)S(1)}, f32[1,2048,128]{2,1,0:T(8,128)}, u32[]{:S(2)}) copy-start(f32[1,2048,128]{2,1,0:T(8,128)} %copy-done.9) | copy-start | bytes 3145732
  229.0 6.2 %collective-permute-start.1 = (f32[3,2048,2]{1,2,0:T(2,128)S(1)}, f32[3,2048,2]{1,2,0:T(2,128)S(1)}, u32[]{:S(2)}, u32[]{:S(2)}) collective-permute-start(f32[3,2048,2]{1,2,0:T(2,128)S(1)} %copy.97), channel_id=1, source_target_pairs={{1,0},{2,1},{3,2},{4,3},{5,4},{6,5},{7,6},{9,8},{10,9},{11,10},{12... | collective-permute-start | bytes 147464 | tf_op jit(solution)/shard_map/ppermute | solution.py:14
  243.4 12.4 %all-to-all-start.5 = ((f32[1,8,64,128]{3,2,0,1:T(8,128)}), f32[1,8,64,128]{3,2,0,1:T(8,128)S(1)}, u32[]{:S(2)}, u32[]{:S(2)}) async-start(f32[1,8,64,128]{3,2,0,1:T(8,128)} %copy.103), calls=%async_computation.6 | async-start | bytes 524288 | tf_op jit(solution)/shard_map/all_to_all | solution.py:136
Sparse Core Ops, SparseCore 0:
  208.5 26.0 reduce-scatter.1
where the time goes:
time: 268 us; the launch traced here: 264 us
  matrix products  110 us (41%)
  waiting for transfers between devices  57.8 us (22%)
  starting transfers between devices  34 us (13%)
  other arithmetic  23.6 us (9%)
  local copies, waits for them, and re-layouts  23.5 us (9%)
  between operations  14.8 us (6%)
    all_to_all x1, waiting for transfers between devices, shards(): lax.all_to_all(long_filter.reshape(dp_count, ctx_count, slab, inner), 'ct...  14 us
    dot_general x3, matrix products, inverse_dft(): jnp.einsum('dqsm,mr->dqsr', spec_real, last_cos, precision=exact_mode)  13.2 us
    dot_general x3, matrix products, inverse_dft(): jnp.einsum('dqsm,mr->dqsr', spec_imag, last_cos, precision=exact_mode)  12.8 us
    all_to_all x1, waiting for transfers between devices, shards(): lax.all_to_all(grad_rows, 'ctx', split_axis=1, concat_axis=1, tiled=True)  11.5 us
    all_to_all x1, waiting for transfers between devices, shards(): lax.all_to_all(gate_rows, 'ctx', split_axis=1, concat_axis=1, tiled=True)  11.1 us
    all_to_all x1, waiting for transfers between devices, shards(): lax.all_to_all(corr_ch, 'ctx', split_axis=1, concat_axis=1, tiled=True)  11 us
    dot_general x3, matrix products, inverse_dft(): jnp.einsum('dqsm,mr->dqsr', spec_imag, last_sin, precision=exact_mode)  10.8 us
    dot_general x3, matrix products, forward_dft(): jnp.einsum('dqp,dpsr->dqsr', first_cos, signal, precision=exact_mode)  10.4 us
  transfers between devices with their start and end apart: 9, of which 7 were waited for; matrix products, arithmetic and copies ran while one was open for 27% of the time, Pallas kernels for 0%

commit v1 on v0

v1 whole, which is shorter than its diff:
```python
import functools
import math

import jax
import jax.numpy as jnp
import numpy as np
from jax import lax
from jax.experimental import pallas as pl
from jax.experimental.pallas import tpu as pltpu
from jax.sharding import PartitionSpec as P

exact_mode = lax.Precision.HIGHEST
f32 = jnp.float32
bf16 = jnp.bfloat16
TABLE_BYTES = 16 * 2**20


def angle_table(rows, cols, period):
    row_index = lax.broadcasted_iota(jnp.int32, (rows, cols), 0)
    col_index = lax.broadcasted_iota(jnp.int32, (rows, cols), 1)
    product = row_index * col_index % period
    return product.astype(jnp.float32) * (2.0 * math.pi / period)


def forward_dft(signal):
    groups = signal.shape[0]
    blocks = signal.shape[1]
    inner = signal.shape[3]
    outer = 2 * blocks
    total = outer * inner
    first_angle = angle_table(outer, blocks, outer)
    first_cos = jnp.broadcast_to(jnp.cos(first_angle), (groups, outer, blocks))
    first_sin = jnp.broadcast_to(-jnp.sin(first_angle), (groups, outer, blocks))
    part_real = jnp.einsum("dqp,dpsr->dqsr", first_cos, signal, precision=exact_mode)
    part_imag = jnp.einsum("dqp,dpsr->dqsr", first_sin, signal, precision=exact_mode)
    twist = angle_table(outer, inner, total)
    twist_cos = jnp.cos(twist)[None, :, None, :]
    twist_sin = jnp.sin(twist)[None, :, None, :]
    mid_real = part_real * twist_cos + part_imag * twist_sin
    mid_imag = part_imag * twist_cos - part_real * twist_sin
    last_angle = angle_table(inner, inner, inner)
    last_cos = jnp.cos(last_angle)
    last_sin = jnp.sin(last_angle)
    out_real = jnp.einsum("dqsr,rm->dqsm", mid_real, last_cos, precision=exact_mode) + jnp.einsum(
        "dqsr,rm->dqsm", mid_imag, last_sin, precision=exact_mode
    )
    out_imag = jnp.einsum("dqsr,rm->dqsm", mid_imag, last_cos, precision=exact_mode) - jnp.einsum(
        "dqsr,rm->dqsm", mid_real, last_sin, precision=exact_mode
    )
    return (out_real, out_imag)


def inverse_dft(spectrum):
    spec_real, spec_imag = spectrum
    groups = spec_real.shape[0]
    outer = spec_real.shape[1]
    inner = spec_real.shape[3]
    blocks = outer // 2
    total = outer * inner
    last_angle = angle_table(inner, inner, inner)
    last_cos = jnp.cos(last_angle)
    last_sin = jnp.sin(last_angle)
    mid_real = jnp.einsum("dqsm,mr->dqsr", spec_real, last_cos, precision=exact_mode) - jnp.einsum(
        "dqsm,mr->dqsr", spec_imag, last_sin, precision=exact_mode
    )
    mid_imag = jnp.einsum("dqsm,mr->dqsr", spec_real, last_sin, precision=exact_mode) + jnp.einsum(
        "dqsm,mr->dqsr", spec_imag, last_cos, precision=exact_mode
    )
    twist = angle_table(outer, inner, total)
    twist_cos = jnp.cos(twist)[None, :, None, :]
    twist_sin = jnp.sin(twist)[None, :, None, :]
    turned_real = mid_real * twist_cos - mid_imag * twist_sin
    turned_imag = mid_real * twist_sin + mid_imag * twist_cos
    first_angle = angle_table(blocks, outer, outer)
    first_cos = jnp.broadcast_to(jnp.cos(first_angle), (groups, blocks, outer))
    first_sin = jnp.broadcast_to(jnp.sin(first_angle), (groups, blocks, outer))
    result = jnp.einsum(
        "dpq,dqsr->dpsr", first_cos, turned_real, precision=exact_mode
    ) - jnp.einsum("dpq,dqsr->dpsr", first_sin, turned_imag, precision=exact_mode)
    return result * (1.0 / total)


def spec_product(left, right):
    return (left[0] * right[0] - left[1] * right[1], left[0] * right[1] + left[1] * right[0])


def conj_product(left, right):
    return (left[0] * right[0] + left[1] * right[1], left[0] * right[1] - left[1] * right[0])


def whole(shape):
    return pl.BlockSpec(shape, lambda k: (0,) * len(shape))


def cost(flops, nbytes):
    return pl.CostEstimate(flops=int(flops), bytes_accessed=int(nbytes), transcendentals=0)


def pick(rows, cols, pairs):
    r = lax.broadcasted_iota(jnp.int32, (rows, cols), 0)
    c = lax.broadcasted_iota(jnp.int32, (rows, cols), 1)
    hit = functools.reduce(jnp.logical_or, [(r == a) & (c == b) for a, b in pairs])
    return jnp.where(hit, 1.0, 0.0).astype(bf16)


def nt(a, b):
    return lax.dot_general(a, b, (((1,), (1,)), ((), ())), preferred_element_type=f32)


def tn(a, b):
    return lax.dot_general(a, b, (((0,), (0,)), ((), ())), preferred_element_type=f32)


def flat(value, rows):
    return value.astype(f32).reshape(rows, value.shape[-1])


def edge_kernel(rows, inner, proj_ref, cot_ref, filt_ref, last_ref, first_ref, filt_out):
    last = jnp.zeros((8, rows), f32)
    first = jnp.zeros((8, rows), f32)
    for m in range(4):
        source = proj_ref[m] if m < 3 else cot_ref[...]
        value = flat(source, rows).astype(bf16)
        if m < 3:
            last += nt(pick(8, inner, [(2 * m, inner - 2), (2 * m + 1, inner - 1)]), value)
        first += nt(pick(8, inner, [(2 * m, 0), (2 * m + 1, 1)]), value)
    last_ref[0] = last.astype(bf16)
    first_ref[0] = first.astype(bf16)
    filt_out[0] = flat(filt_ref[...], rows).astype(bf16)


def activations(rows, inner, proj_ref, prev, taps):
    spots = []
    for m in range(3):
        at = 2 * inner * m
        spots += [(2 * m + 1, at), (2 * m, at + inner), (2 * m + 1, at + inner + 1)]
    placed = tn(prev, pick(8, 6 * inner, spots))
    lane = lax.broadcasted_iota(jnp.int32, (rows, inner), 1)
    act = []
    for m in range(3):
        x = flat(proj_ref[m], rows)
        one = placed[:, 2 * inner * m : 2 * inner * m + inner]
        two = placed[:, 2 * inner * m + inner : 2 * inner * (m + 1)]
        x1 = jnp.where(lane < 1, one, pltpu.roll(x, 1, 1))
        x2 = jnp.where(lane < 2, two, pltpu.roll(x, 2, 1))
        act.append(taps[m][:, 0:1] * x + taps[m][:, 1:2] * x1 + taps[m][:, 2:3] * x2)
    return act


def gate_kernel(rows, inner, proj_ref, cot_ref, prev_ref, taps_ref, gate_ref, grad_ref):
    taps = [flat(taps_ref[m], rows) for m in range(3)]
    first, second, value = activations(rows, inner, proj_ref, prev_ref[0], taps)
    gate_ref[0] = (first * value).astype(bf16)
    grad_ref[0] = (flat(cot_ref[...], rows) * second).astype(bf16)


def split(value):
    high = value.astype(bf16)
    low = (value - high.astype(f32)).astype(bf16)
    return jnp.concatenate([high, low], axis=0)


ROOT_HALF = math.sqrt(0.5)


def spectrum(x_ref, small_ref, large_ref, spec_ref):
    n, rows, inner = x_ref.shape
    per = n // 4
    q = per * inner
    x0, x1, x2, x3 = (
        jnp.concatenate([x_ref[p * per + i].astype(f32) for i in range(per)], axis=1) for p in range(4)
    )

    def put(at, value, table):
        both = jnp.dot(split(value), table, preferred_element_type=f32)
        spec_ref[:, at * q : at * q + table.shape[1]] = both[:rows] + both[rows:]

    even, odd = x0 + x2, x1 + x3
    put(0, even + odd, small_ref[0])
    put(1, even - odd, small_ref[1])
    put(4, jnp.concatenate([x0 - x2, x3 - x1], axis=1), large_ref[1])
    turn_a, turn_b = (x1 - x3) * ROOT_HALF, odd * ROOT_HALF
    put(2, jnp.concatenate([x0 + turn_a, -x2 - turn_b], axis=1), large_ref[0])
    put(6, jnp.concatenate([x0 - turn_a, x2 - turn_b], axis=1), large_ref[2])


def product_inverse(a_ref, b_ref, conj, small_ref, large_ref, q):
    rows = a_ref.shape[0]

    def back(at, width, table):
        half = width // 2
        start = at * q
        ar, ai = a_ref[:, start : start + half], a_ref[:, start + half : start + width]
        br, bi = b_ref[:, start : start + half], b_ref[:, start + half : start + width]
        rr, ii, ri, ir = ar * br, ai * bi, ar * bi, ai * br
        re, im = (rr + ii, ri - ir) if conj else (rr - ii, ri + ir)
        if at == 0:
            lane = lax.broadcasted_iota(jnp.int32, (rows, half), 1)
            re = jnp.where(lane == 0, 0.5 * rr, re)
            im = jnp.where(lane == 0, 0.5 * ii, im)
        scale = 2.0 / (8 * q)
        both = jnp.concatenate([re * scale, im * scale], axis=1).astype(bf16)
        return nt(both, table)

    v0 = back(0, q, small_ref[0])
    v4 = back(1, q, small_ref[1])
    u2 = back(4, 2 * q, large_ref[1])
    r2, i2 = u2[:, :q], u2[:, q:]
    e0, e1, e2, e3 = v0 + v4 + r2, v0 - v4 - i2, v0 + v4 - r2, v0 - v4 + i2
    u1 = back(2, 2 * q, large_ref[0])
    u3 = back(6, 2 * q, large_ref[2])
    r1, i1, r3, i3 = u1[:, :q], u1[:, q:], u3[:, :q], u3[:, q:]
    o1 = (r1 - i1 - r3 - i3) * ROOT_HALF
    o3 = (r3 - i3 - r1 - i1) * ROOT_HALF
    return e0 + r1 + r3, e1 + o1, e2 - i1 + i3, e3 + o3


def blocks_of(quarters, inner):
    per = quarters[0].shape[1] // inner
    return [part[:, i * inner : (i + 1) * inner] for part in quarters for i in range(per)]


def store_result(out_ref, blocks, rows, inner):
    lanes = -(-rows // 128) * 128
    rounded = [b.astype(bf16) for b in blocks]
    for k, block in enumerate(rounded):
        out_ref[k, :rows] = block
        if k + 1 < len(rounded):
            after = rounded[k + 1]
            if lanes > rows:
                after = jnp.concatenate([after, jnp.zeros((lanes - rows, inner), bf16)], axis=0)
            tail = nt(pick(8, inner, [(0, 0), (1, 1)]), after)
        else:
            tail = jnp.zeros((8, lanes), f32)
        parts = [tail[:, i : i + 128] for i in range(0, lanes, 128)]
        out_ref[k, rows : rows + 8 * len(parts)] = jnp.concatenate(parts, axis=0).astype(bf16)


def filter_kernel(filt_ref, small_ref, large_ref, spec_ref):
    spectrum(filt_ref, small_ref, large_ref, spec_ref)


def conv_kernel(gate_ref, filt_spec, small_ref, large_ref, gate_spec, out_ref):
    n, rows, inner = gate_ref.shape
    spectrum(gate_ref, small_ref, large_ref, gate_spec)
    parts = product_inverse(filt_spec, gate_spec, False, small_ref, large_ref, n * inner // 4)
    store_result(out_ref, blocks_of(parts, inner), rows, inner)


def fgrad_kernel(grad_ref, gate_spec, small_ref, large_ref, grad_spec, out_ref):
    n, rows, inner = grad_ref.shape
    spectrum(grad_ref, small_ref, large_ref, grad_spec)
    parts = product_inverse(gate_spec, grad_spec, True, small_ref, large_ref, n * inner // 4)
    groups, _, slab, _ = out_ref.shape
    for k, block in enumerate(blocks_of(parts, inner)):
        for d in range(groups):
            out_ref[d, k] = block[d * slab : (d + 1) * slab].astype(out_ref.dtype)


def corr_kernel(grad_spec, filt_spec, small_ref, large_ref, own_ref, got_ref, out_ref):
    n, slab, inner = own_ref.shape
    rows = grad_spec.shape[0]
    parts = product_inverse(filt_spec, grad_spec, True, small_ref, large_ref, n * inner // 4)
    store_result(out_ref, blocks_of(parts, inner), rows, inner)
    at = out_ref.shape[1] - slab
    for k in range(n):
        total = own_ref[k].astype(f32)
        for e in range(got_ref.shape[0]):
            total = total + got_ref[e, k].astype(f32)
        out_ref[k, at:] = total.astype(bf16)


def result_kernel(
    rows,
    inner,
    scale,
    proj_ref,
    cot_ref,
    prev_ref,
    own_ref,
    next_ref,
    taps_ref,
    skip_ref,
    row_ref,
    conv_ref,
    corr_ref,
    out_ref,
    pg_ref,
    fg_ref,
):
    taps = [flat(taps_ref[m], rows) for m in range(3)]
    skip = flat(skip_ref[...], rows)
    first, second, value = activations(rows, inner, proj_ref, prev_ref[0], taps)
    upstream = flat(cot_ref[...], rows)
    gate = (first * value).astype(bf16).astype(f32)
    grad = (upstream * second).astype(bf16).astype(f32)
    mixed = conv_ref[0, :rows].astype(f32) + skip * gate
    out_ref[...] = (second * mixed).astype(bf16).reshape(out_ref.shape)
    gate_grad = corr_ref[0, :rows].astype(f32) + skip * grad
    act_grad = (gate_grad * value, upstream * mixed, gate_grad * first)

    lanes = -(-rows // 128) * 128

    def tail_of(ref):
        parts = [ref[0, rows + 8 * i : rows + 8 * i + 8].astype(f32) for i in range(lanes // 128)]
        return jnp.concatenate(parts, axis=1)[:, :rows]

    conv_tail, corr_tail = tail_of(conv_ref), tail_of(corr_ref)
    own = own_ref[0].astype(f32)
    after = next_ref[0].astype(f32)
    param = row_ref[0]
    spare = []
    for t in range(2):
        ahead = []
        for m in range(3):
            history = (after[2 * m + t : 2 * m + t + 1],) + (
                (own[2 * m + 1 : 2 * m + 2], own[2 * m : 2 * m + 1])
                if t == 0
                else (after[2 * m : 2 * m + 1], own[2 * m + 1 : 2 * m + 2])
            )
            ahead.append(
                param[3 * m : 3 * m + 1] * history[0]
                + param[3 * m + 1 : 3 * m + 2] * history[1]
                + param[3 * m + 2 : 3 * m + 3] * history[2]
            )
        above = after[6 + t : 7 + t]
        keep = param[9:10]
        gate_t = (ahead[0] * ahead[2]).astype(bf16).astype(f32)
        grad_t = (above * ahead[1]).astype(bf16).astype(f32)
        mixed_t = conv_tail[t : t + 1] + keep * gate_t
        gate_grad_t = corr_tail[t : t + 1] + keep * grad_t
        spare.append((gate_grad_t * ahead[2], above * mixed_t, gate_grad_t * ahead[0]))
    line = lax.broadcasted_iota(jnp.int32, (8, rows), 0)
    beyond = jnp.zeros((8, rows), f32)
    for m in range(3):
        for t in range(2):
            beyond = jnp.where(line == 2 * m + t, spare[t][m], beyond)
    high = beyond.astype(bf16)
    low = (beyond - high.astype(f32)).astype(bf16)
    spots = []
    for m in range(3):
        at = 2 * inner * m
        spots += [(2 * m, at + inner - 1), (2 * m, at + 2 * inner - 2), (2 * m + 1, at + 2 * inner - 1)]
    where_to = pick(8, 6 * inner, spots)
    placed = tn(high, where_to) + tn(low, where_to)
    lane = lax.broadcasted_iota(jnp.int32, (rows, inner), 1)
    for m in range(3):
        x = act_grad[m]
        one = placed[:, 2 * inner * m : 2 * inner * m + inner]
        two = placed[:, 2 * inner * m + inner : 2 * inner * (m + 1)]
        x1 = jnp.where(lane >= inner - 1, one, pltpu.roll(x, inner - 1, 1))
        x2 = jnp.where(lane >= inner - 2, two, pltpu.roll(x, inner - 2, 1))
        back = taps[m][:, 0:1] * x + taps[m][:, 1:2] * x1 + taps[m][:, 2:3] * x2
        pg_ref[m] = back.astype(bf16).reshape(pg_ref.shape[1:])
    slab = fg_ref.shape[1]
    fg_ref[0] = corr_ref[0, corr_ref.shape[1] - slab :].astype(f32) * scale


def dft_tables(q):
    r = np.arange(q)[:, None]
    step = 2.0 * np.pi / (8 * q)

    def angle(residue, count):
        return (r * (residue + 8 * np.arange(count)[None, :]) % (8 * q)) * step

    small = []
    for residue in (0, 4):
        a = angle(residue, q // 2)
        table = np.concatenate([np.cos(a), -np.sin(a)], axis=1)
        if residue == 0:
            table[:, q // 2] = 1.0 - 2.0 * (np.arange(q) % 2)
        small.append(table)
    large = []
    for residue in (1, 2, 3):
        a = angle(residue, q)
        large.append(np.block([[np.cos(a), -np.sin(a)], [np.sin(a), np.cos(a)]]))
    return (np.stack(small).astype(jnp.bfloat16), np.stack(large).astype(jnp.bfloat16))


def shards(projections, short_filter, long_filter, skip_gain, cotangent):
    groups = lax.axis_size("dp")
    n = lax.axis_size("ctx")
    channels = projections.shape[2]
    inner = projections.shape[3]
    slab = channels // (groups * n)
    rows = groups * slab
    length = inner * n
    q = length // 4
    tail_rows = 8 * -(-rows // 128)

    proj = projections.reshape(3, groups, n, slab, inner)
    cot = cotangent.reshape(groups, n, slab, inner)
    filt = long_filter.reshape(groups, n, slab, inner)
    taps = short_filter.reshape(3, groups, n, slab, 3)
    skip = skip_gain.reshape(groups, n, slab, 1)
    row_taps = jnp.transpose(taps, (2, 0, 4, 1, 3)).reshape(n, 9, rows)
    row_skip = jnp.transpose(skip, (1, 3, 0, 2)).reshape(n, 1, rows)
    row_param = jnp.concatenate([row_taps, row_skip, jnp.zeros((n, 6, rows), f32)], axis=1)

    proj_spec = pl.BlockSpec((3, groups, None, slab, inner), lambda k: (0, 0, k, 0, 0))
    cot_spec = pl.BlockSpec((groups, None, slab, inner), lambda k: (0, k, 0, 0))
    taps_spec = pl.BlockSpec((3, groups, None, slab, 3), lambda k: (0, 0, k, 0, 0))
    skip_spec = pl.BlockSpec((groups, None, slab, 1), lambda k: (0, k, 0, 0))
    edge_spec = pl.BlockSpec((1, 8, rows), lambda k: (k, 0, 0))
    row_spec = pl.BlockSpec((1, 16, rows), lambda k: (k, 0, 0))

    def block_spec(count):
        return pl.BlockSpec((1, count, inner), lambda k: (k, 0, 0))

    def block_shape(count):
        return jax.ShapeDtypeStruct((n, count, inner), bf16)

    edge_shape = jax.ShapeDtypeStruct((n, 8, rows), bf16)
    size = channels * inner

    last, first, filt_rows = pl.pallas_call(
        functools.partial(edge_kernel, rows, inner),
        grid=(n,),
        in_specs=[proj_spec, cot_spec, cot_spec],
        out_specs=[edge_spec, edge_spec, block_spec(rows)],
        out_shape=[edge_shape, edge_shape, block_shape(rows)],
        cost_estimate=cost(64 * size, 14 * size),
        name="edges",
    )(proj, cot, filt)
    forth = [(i, i + 1) for i in range(n - 1)]
    prev = lax.ppermute(last, "ctx", forth)
    after = lax.ppermute(first, "ctx", [(b, a) for a, b in forth])

    gate, grad = pl.pallas_call(
        functools.partial(gate_kernel, rows, inner),
        grid=(n,),
        in_specs=[proj_spec, cot_spec, edge_spec, taps_spec],
        out_specs=[block_spec(rows), block_spec(rows)],
        out_shape=[block_shape(rows), block_shape(rows)],
        cost_estimate=cost(2000 * size, 16 * size),
        name="gates",
    )(proj, cot, prev, taps)

    def across(value):
        return lax.all_to_all(value, "ctx", split_axis=0, concat_axis=0, tiled=True)

    filt_ch = across(filt_rows)
    gate_ch = across(gate)
    grad_ch = across(grad)

    me = lax.axis_index("dp")
    scale = 1.0 / math.sqrt(groups * length)

    def from_others(pieces):
        got = []
        for e in range(1, groups):
            piece = lax.dynamic_index_in_dim(pieces, lax.rem(me + e, groups), 0, keepdims=False)
            got.append(lax.ppermute(piece, "dp", [(i, (i + e) % groups) for i in range(groups)]))
        return lax.dynamic_index_in_dim(pieces, me, 0, keepdims=False), jnp.stack(got)

    if n % 4 == 0 and 2 * (14 * q * q) <= TABLE_BYTES:
        small, large = (jnp.asarray(t) for t in dft_tables(q))
        spec_shape = jax.ShapeDtypeStruct((rows, 8 * q), f32)
        dft = 2 * rows * 14 * q * q

        def call(kernel, outs, factor, name, *args):
            return pl.pallas_call(
                kernel,
                out_shape=outs,
                cost_estimate=cost(factor * dft, 30 * rows * q * 4),
                name=name,
            )(*args)

        filt_spec = call(filter_kernel, spec_shape, 2, "filter_spectrum", filt_ch, small, large)
        gate_spec, conv_send = call(
            conv_kernel, [spec_shape, block_shape(rows + tail_rows)], 3, "conv", gate_ch, filt_spec, small, large
        )
        conv_pos = across(conv_send)
        grad_spec, pieces = call(
            fgrad_kernel,
            [spec_shape, jax.ShapeDtypeStruct((groups, n, slab, inner), bf16)],
            3,
            "filter_gradient",
            grad_ch,
            gate_spec,
            small,
            large,
        )
        own, got = from_others(pieces)
        corr_send = call(
            corr_kernel,
            block_shape(rows + tail_rows + slab),
            1,
            "corr",
            grad_spec,
            filt_spec,
            small,
            large,
            own,
            got,
        )
        corr_pos = across(corr_send)
    else:

        def grouped(value):
            return jnp.transpose(value.reshape(n, groups, slab, inner), (1, 0, 2, 3)).astype(f32)

        filt_spec = forward_dft(grouped(filt_ch))
        gate_spec = forward_dft(grouped(gate_ch))
        grad_spec = forward_dft(grouped(grad_ch))

        def returned(spec):
            value = jnp.transpose(inverse_dft(spec), (1, 0, 2, 3)).reshape(n, rows, inner).astype(bf16)
            tail = jnp.transpose(value[1:, :, 0:2], (0, 2, 1))
            lanes = 16 * tail_rows
            tail = jnp.pad(tail, ((0, 1), (0, 6), (0, lanes - rows)))
            tail = jnp.transpose(tail.reshape(n, 8, lanes // 128, 128), (0, 2, 1, 3)).reshape(n, tail_rows, 128)
            return jnp.concatenate([value, tail], axis=1)

        own, got = from_others(inverse_dft(conj_product(gate_spec, grad_spec)).astype(bf16))
        total = (own.astype(f32) + jnp.sum(got.astype(f32), axis=0)).astype(bf16)
        conv_pos = across(returned(spec_product(filt_spec, gate_spec)))
        corr_pos = across(jnp.concatenate([returned(conj_product(filt_spec, grad_spec)), total], axis=1))

    layer_out, proj_grad, filter_grad = pl.pallas_call(
        functools.partial(result_kernel, rows, inner, scale),
        grid=(n,),
        in_specs=[
            proj_spec,
            cot_spec,
            edge_spec,
            edge_spec,
            edge_spec,
            taps_spec,
            skip_spec,
            row_spec,
            block_spec(rows + tail_rows),
            block_spec(rows + tail_rows + slab),
        ],
        out_specs=[cot_spec, proj_spec, pl.BlockSpec((1, slab, inner), lambda k: (k, 0, 0))],
        out_shape=[
            jax.ShapeDtypeStruct(cot.shape, bf16),
            jax.ShapeDtypeStruct(proj.shape, bf16),
            jax.ShapeDtypeStruct((n, slab, inner), f32),
        ],
        cost_estimate=cost(2000 * size, 24 * size),
        name="results",
    )(proj, cot, prev, last, after, taps, skip, row_param, conv_pos, corr_pos)
    return (
        layer_out.reshape(1, channels, inner),
        proj_grad.reshape(1, 3, channels, inner),
        filter_grad.reshape(n * slab, inner),
    )


def solution(mesh):
    placed = (P("dp", None, None, "ctx"), P(), P(None, "ctx"), P(), P("dp", None, "ctx"))
    return jax.shard_map(
        shards,
        mesh=mesh,
        in_specs=placed,
        out_specs=(P("dp", None, "ctx"), P("dp", None, None, "ctx"), P("dp", "ctx")),
        check_vma=False,
    )
```

time: 268 us -> 135 us (0.50); the launches traced: 264 us -> 134 us
  matrix products: 110 us -> 0 us
  Pallas kernels: 0 us -> 44.7 us
  waiting for transfers between devices: 57.8 us -> 24 us
  blocking collectives: 0 us -> 26.9 us
  other arithmetic: 23.6 us -> 1.52 us
  local copies, waits for them, and re-layouts: 23.5 us -> 7.69 us
  between operations: 14.8 us -> 0.78 us
  starting transfers between devices: 34 us -> 28.1 us
    dot_general x36 -> x0, matrix products: 110 us -> none  [the longest x3 13.2 us: inverse_dft(): jnp.einsum('dqsm,mr->dqsr', spec_real, last_cos, precision=exact_mode)]
    pallas_call x0 -> x7, Pallas kernels: none -> 44.7 us  [the longest x4 19.1 us: call(): pl.pallas_call(kernel, out_shape=outs, cost_estimate=cost(factor * dft, 3...]
    all_to_all x6 -> x4, waiting for transfers between devices: 51.7 us -> 16.6 us  [across(): return lax.all_to_all(value, 'ctx', split_axis=0, concat_axis=0, tiled=True)]
    all_to_all x0 -> x1, blocking collectives: none -> 26.9 us  [across(): return lax.all_to_all(value, 'ctx', split_axis=0, concat_axis=0, tiled=True)]
    broadcast_in_dim x1 -> x0, other arithmetic: 8.95 us -> none  [shards(): return (layer_out[None], proj_back.astype(jnp.bfloat16)[None], filter_grad)]
    all_to_all x6 -> x4, starting transfers between devices: 27.3 us -> 20.9 us  [across(): return lax.all_to_all(value, 'ctx', split_axis=0, concat_axis=0, tiled=True)]
    add x1 -> x0, other arithmetic: 4.67 us -> none  [shards(): tap_zero * extended[:, :, 2:] + tap_one * extended[:, :, 1:inner + 1]]
    all_to_all x2 -> x0, local copies, waits for them, and re-layouts: 3.87 us -> none  [the longest x1 2.4 us: shards(): lax.all_to_all(conv_ch, 'ctx', split_axis=1, concat_axis=1, tiled=True)]
  transfers between devices with their start and end apart: 9 -> 9, of which waited for: 7 -> 6; matrix products, arithmetic and copies ran while one was open for 27% -> 6% of each run, Pallas kernels for 0% -> 20%
where the time goes in v1:
time: 135 us; the launch traced here: 134 us
  Pallas kernels  44.7 us (33%)
  starting transfers between devices  28.1 us (21%)
  blocking collectives  26.9 us (20%)
  waiting for transfers between devices  24 us (18%)
  local copies, waits for them, and re-layouts  7.69 us (6%)
  other arithmetic  1.52 us (1%)
    all_to_all x1, blocking collectives, across(): return lax.all_to_all(value, 'ctx', split_axis=0, concat_axis=0, tiled=True)  26.9 us
    all_to_all x4, starting transfers between devices, across(): return lax.all_to_all(value, 'ctx', split_axis=0, concat_axis=0, tiled=True)  20.9 us
    pallas_call x4, Pallas kernels, call(): pl.pallas_call(kernel, out_shape=outs, cost_estimate=cost(factor * dft, 3...  19.1 us
    all_to_all x4, waiting for transfers between devices, across(): return lax.all_to_all(value, 'ctx', split_axis=0, concat_axis=0, tiled=True)  16.6 us
    pallas_call x1, Pallas kernels, shards(): pl.pallas_call(functools.partial(result_kernel, rows, inner, scale), grid...  10.9 us
    pallas_call x1, Pallas kernels, shards(): pl.pallas_call(functools.partial(gate_kernel, rows, inner), grid=(n,), in...  8.11 us
    pallas_call x1, Pallas kernels, shards(): pl.pallas_call(functools.partial(edge_kernel, rows, inner), grid=(n,), in...  6.59 us
    ppermute x3, waiting for transfers between devices, from_others(): lax.ppermute(piece, 'dp', [(i, (i + e) % groups) for i in range(groups)])  5.29 us
  transfers between devices with their start and end apart: 9, of which 6 were waited for; matrix products, arithmetic and copies ran while one was open for 6% of the time, Pallas kernels for 20%

profile of v1, /device:TPU:0, one launch (start us, length us, event | category | flops | bytes accessed | tf_op | source)
XLA Modules:
  0.0 133.6 jit_solution(5483388932513007904)
XLA Ops:
  0.6 0.0 copy-start.4
  0.6 6.6 %edges.1 = (bf16[8,8,256]{2,1,0:T(8,128)(2,1)}, bf16[8,8,256]{2,1,0:T(8,128)(2,1)}, bf16[8,256,128]{2,1,0:T(8,128)(2,1)}) custom-call(bf16[3,4,8,64,128]{4,3,2,1,0:T(8,128)(2,1)} %bitcast.26, bf16[4,8,64,128]{3,2,1,0:T(8,128)(2,1)} %bitcast.29, f32[4,8,64,128]{3,2,1,0:T(8,128)} %bitcast.32), custom_call_target="tpu_custom_call" | custom-call | flops 16777216 | bytes 3670016 | tf_op jit(solution)/shard_map/edges/pallas_call | solution.py:416
  7.2 7.3 %all-to-all-start.1 = ((bf16[8,256,128]{2,1,0:T(8,128)(2,1)}), bf16[8,256,128]{2,1,0:T(8,128)(2,1)S(1)}, u32[]{:S(2)}, u32[]{:S(2)}) async-start(bf16[8,256,128]{2,1,0:T(8,128)(2,1)} %get-tuple-element.18), calls=%async_computation.1 | async-start | bytes 1048576 | tf_op jit(solution)/shard_map/all_to_all | solution.py:440
  14.5 3.9 %collective-permute-start = (bf16[8,8,256]{2,1,0:T(8,128)(2,1)}, bf16[8,8,256]{2,1,0:T(8,128)(2,1)S(1)}, u32[]{:S(2)}, u32[]{:S(2)}) collective-permute-start(bf16[8,8,256]{2,1,0:T(8,128)(2,1)} %get-tuple-element.15.own_ref), channel_id=1, source_target_pairs={{0,1},{1,2},{2,3},{3,4},{4,5},{5,6},{6,7},{8,9},{9,10},{10,11},{11... | collective-permute-start | bytes 98312 | tf_op jit(solution)/shard_map/ppermute | solution.py:426
  18.5 0.0 copy-done.4
  18.5 2.2 %copy.13 = f32[3,2048,3]{2,1,0:T(8,128)} copy(f32[3,2048,3]{1,2,0:T(4,128)S(1)} %copy-done.4) | data formatting | bytes 147456 | tf_op args[1]
  20.7 0.0 collective-permute-done.prev_ref
  20.7 0.0 copy-start.3
  20.7 0.6 copy-done.3
  21.3 8.1 %gates.1 = (bf16[8,256,128]{2,1,0:T(8,128)(2,1)}, bf16[8,256,128]{2,1,0:T(8,128)(2,1)}) custom-call(bf16[3,4,8,64,128]{4,3,2,1,0:T(8,128)(2,1)} %bitcast.27, bf16[4,8,64,128]{3,2,1,0:T(8,128)(2,1)} %bitcast.30, bf16[8,8,256]{2,1,0:T(8,128)(2,1)} %copy-done.3, f32[3,4,8,64,3]{4,3,2,1,0:T(8,128)} %bitcast.23), custom_call_target="tpu_custom_call" | custom-call | flops 524288000 | bytes 4194304 | tf_op jit(solution)/shard_map/gates/pallas_call | solution.py:429
  29.4 0.0 all-to-all-done.1.filt_ref
  29.4 0.0 copy-start.1
  29.4 26.9 %all_to_all.25.gate_ref = bf16[8,256,128]{2,1,0:T(8,128)(2,1)} all-to-all(bf16[8,256,128]{2,1,0:T(8,128)(2,1)} %get-tuple-element.17), channel_id=1, replica_groups=mesh['dp'=4,'ctx'=8] {'ctx'}, dimensions={0} | all-to-all | bytes 1048576 | tf_op jit(solution)/shard_map/all_to_all | solution.py:440
  56.4 3.5 %all-to-all-start.3 = ((bf16[8,256,128]{2,1,0:T(8,128)(2,1)}), bf16[8,256,128]{2,1,0:T(8,128)(2,1)S(1)}, u32[]{:S(2)}, u32[]{:S(2)}) async-start(bf16[8,256,128]{2,1,0:T(8,128)(2,1)} %get-tuple-element.20), calls=%async_computation.3 | async-start | bytes 1048576 | tf_op jit(solution)/shard_map/all_to_all | solution.py:440
  59.9 0.0 copy-done.1
  59.9 4.2 %filter_spectrum.1.filt_spec = f32[256,2048]{1,0:T(8,128)} custom-call(bf16[8,256,128]{2,1,0:T(8,128)(2,1)} %copy-done.1, bf16[2,256,256]{2,1,0:T(8,128)(2,1)} %constant.36.clone.small_ref, bf16[3,512,512]{2,1,0:T(8,128)(2,1)} %constant.37.clone.large_ref), custom_call_target="tpu_custom_call" | custom-call | flops 939524096 | bytes 7864320 | tf_op jit(solution)/shard_map/filter_spectrum/pallas_call | solution.py:462
  64.1 5.1 %conv.1 = (f32[256,2048]{1,0:T(8,128)}, bf16[8,272,128]{2,1,0:T(8,128)(2,1)}) custom-call(bf16[8,256,128]{2,1,0:T(8,128)(2,1)} %all_to_all.25.gate_ref, f32[256,2048]{1,0:T(8,128)} %filter_spectrum.1.filt_spec, bf16[2,256,256]{2,1,0:T(8,128)(2,1)} %constant.36.clone.small_ref, bf16[3,512,512]{2,1,0:T(8,128)(2,1)} %constant.37.clone.large_ref), custom_call_target="tpu_custom_call" | custom-call | flops 1409286144 | bytes 7864320 | tf_op jit(solution)/shard_map/conv/pallas_call | solution.py:462
  69.2 4.9 %all-to-all-done.3.grad_ref = bf16[8,256,128]{2,1,0:T(8,128)(2,1)S(1)} async-done(((bf16[8,256,128]{2,1,0:T(8,128)(2,1)}), bf16[8,256,128]{2,1,0:T(8,128)(2,1)S(1)}, u32[]{:S(2)}, u32[]{:S(2)}) %all-to-all-start.3) | async-done | bytes 524320 | tf_op jit(solution)/shard_map/all_to_all | solution.py:440
  74.0 0.0 copy-start.2
  74.0 4.2 %all-to-all-start.2 = ((bf16[8,272,128]{2,1,0:T(8,128)(2,1)}), bf16[8,272,128]{2,1,0:T(8,128)(2,1)}, u32[]{:S(2)}, u32[]{:S(2)}) async-start(bf16[8,272,128]{2,1,0:T(8,128)(2,1)} %get-tuple-element.19), calls=%async_computation.2 | async-start | bytes 1114112 | tf_op jit(solution)/shard_map/all_to_all | solution.py:440
  78.2 0.0 copy-done.2
  78.3 5.0 %filter_gradient.1 = (f32[256,2048]{1,0:T(8,128)}, bf16[4,8,64,128]{3,2,1,0:T(8,128)(2,1)}) custom-call(bf16[8,256,128]{2,1,0:T(8,128)(2,1)} %copy-done.2, f32[256,2048]{1,0:T(8,128)} %get-tuple-element.21.gate_spec, bf16[2,256,256]{2,1,0:T(8,128)(2,1)} %constant.36.clone.small_ref, bf16[3,512,512]{2,1,0:T(8,128)(2,1)} %constant.37.clone.large_ref), custom_call_target="tpu_custom_call" | custom-call | flops 1409286144 | bytes 7864320 | tf_op jit(solution)/shard_map/filter_gradient/pallas_call | solution.py:462
  83.2 1.8 %dynamic-slice_bitcast_fusion.2 = (bf16[8,64,128]{2,1,0:T(8,128)(2,1)S(1)}, bf16[8,64,128]{2,1,0:T(8,128)(2,1)S(1)}, bf16[8,64,128]{2,1,0:T(8,128)(2,1)S(1)}, bf16[8,64,128]{2,1,0:T(8,128)(2,1)}) fusion(bf16[4,8,64,128]{3,2,1,0:T(8,128)(2,1)} %get-tuple-element.23, s32[]{:T(128)S(6)} %select_n.14, s32[]{:T(128)S(6)} %select_n.16, s32[]{:T(128)S(6)} %select_n.15, ...), kind=kLoop, calls=%fused_computation.4 | loop fusion | bytes 1048592 | tf_op jit(solution)/shard_map/jit(dynamic_index_in_dim)/squeeze | solution.py:452
  85.0 1.5 %collective-permute-start.3 = (bf16[8,64,128]{2,1,0:T(8,128)(2,1)S(1)}, bf16[8,64,128]{2,1,0:T(8,128)(2,1)S(1)}, u32[]{:S(2)}, u32[]{:S(2)}) collective-permute-start(bf16[8,64,128]{2,1,0:T(8,128)(2,1)S(1)} %get-tuple-element.29), channel_id=1, source_target_pairs={{0,16},{8,24},{16,0},{24,8},{1,17},{9,25},{17,1},{25,9},{2,18},{10... | collective-permute-start | bytes 393224 | tf_op jit(solution)/shard_map/ppermute | solution.py:453
  86.5 0.0 collective-permute-start.4
  86.5 0.5 collective-permute-start.2
  87.0 3.4 %collective-permute-done.3 = bf16[8,64,128]{2,1,0:T(8,128)(2,1)S(1)} collective-permute-done((bf16[8,64,128]{2,1,0:T(8,128)(2,1)S(1)}, bf16[8,64,128]{2,1,0:T(8,128)(2,1)S(1)}, u32[]{:S(2)}, u32[]{:S(2)}) %collective-permute-start.3) | collective-permute-done | bytes 131104 | tf_op jit(solution)/shard_map/ppermute | solution.py:453
  90.4 1.3 collective-permute-done.4
  91.7 0.5 collective-permute-done.2
  92.3 0.8 pad_maximum_fusion.got_ref
  93.1 0.0 copy-start.7
  93.1 0.0 copy-start
  93.1 4.8 %corr.1 = bf16[8,336,128]{2,1,0:T(8,128)(2,1)} custom-call(f32[256,2048]{1,0:T(8,128)} %get-tuple-element.22.grad_spec, f32[256,2048]{1,0:T(8,128)} %filter_spectrum.1.filt_spec, bf16[2,256,256]{2,1,0:T(8,128)(2,1)} %constant.36.clone.small_ref, bf16[3,512,512]{2,1,0:T(8,128)(2,1)} %constant.37.clone.large_ref, ...), custom_call_target="tpu_custom_call" | custom-call | flops 469762048 | bytes 7864320 | tf_op jit(solution)/shard_map/corr/pallas_call | solution.py:462
  97.9 0.0 all-to-all-done.2.conv_ref
  97.9 5.9 %all-to-all-start.4 = ((bf16[8,336,128]{2,1,0:T(8,128)(2,1)}), bf16[8,336,128]{2,1,0:T(8,128)(2,1)}, u32[]{:S(2)}, u32[]{:S(2)}) async-start(bf16[8,336,128]{2,1,0:T(8,128)(2,1)} %corr.1), calls=%async_computation.4 | async-start | bytes 1376256 | tf_op jit(solution)/shard_map/all_to_all | solution.py:440
  103.8 0.0 copy-start.6
  103.8 0.0 copy-done.7
  103.8 1.3 collective-permute-start.1
  105.1 0.0 copy-done
  105.1 1.3 copy.18
  106.4 0.2 reshape.46
  106.6 0.0 copy-done.6
  106.6 0.1 reshape.40
  106.6 0.1 reshape.42
  106.7 0.1 pad.5.clone
  106.8 0.7 maximum_maximum_fusion.row_ref
  107.5 1.4 %copy.17.skip_ref = f32[4,8,64,1]{3,2,1,0:T(8,128)} copy(f32[4,8,64,1]{2,1,0,3:T(8,128)S(1)} %reshape.40) | data formatting | bytes 16384 | tf_op jit(solution)/shard_map/reshape | solution.py:395
  108.9 2.1 %collective-permute-done.1.next_ref = bf16[8,8,256]{2,1,0:T(8,128)(2,1)S(1)} collective-permute-done((bf16[8,8,256]{2,1,0:T(8,128)(2,1)S(1)}, bf16[8,8,256]{2,1,0:T(8,128)(2,1)S(1)}, u32[]{:S(2)}, u32[]{:S(2)}) %collective-permute-start.1) | collective-permute-done | bytes 32800 | tf_op jit(solution)/shard_map/ppermute | solution.py:427
  111.0 0.0 copy-start.5
  111.0 11.7 %all-to-all-done.4.corr_ref = bf16[8,336,128]{2,1,0:T(8,128)(2,1)} async-done(((bf16[8,336,128]{2,1,0:T(8,128)(2,1)}), bf16[8,336,128]{2,1,0:T(8,128)(2,1)}, u32[]{:S(2)}, u32[]{:S(2)}) %all-to-all-start.4) | async-done | bytes 688160 | tf_op jit(solution)/shard_map/all_to_all | solution.py:440
  122.7 0.0 copy-done.5
  122.7 10.9 %results.1 = (bf16[4,8,64,128]{3,2,1,0:T(8,128)(2,1)}, bf16[3,4,8,64,128]{4,3,2,1,0:T(8,128)(2,1)}, f32[8,64,128]{2,1,0:T(8,128)}) custom-call(bf16[3,4,8,64,128]{4,3,2,1,0:T(8,128)(2,1)} %bitcast.28, bf16[4,8,64,128]{3,2,1,0:T(8,128)(2,1)} %bitcast.31, bf16[8,8,256]{2,1,0:T(8,128)(2,1)} %copy-done.3, bf16[8,8,256]{2,1,0:T(8,128)(2,1)} %get-tuple-element.15.own_ref, ...), custom_call_target="tpu_custom_call" | custom-call | flops 524288000 | bytes 6291456 | tf_op jit(solution)/shard_map/results/pallas_call | solution.py:520
  (2 shorter events, 0.0 us)
Async XLA Ops:
  0.6 17.8 %copy-start.4 = (f32[3,2048,3]{1,2,0:T(4,128)S(1)}, f32[3,2048,3]{1,2,0:T(4,128)}, u32[]{:S(2)}) copy-start(f32[3,2048,3]{1,2,0:T(4,128)} %param.8) | copy-start | bytes 221188
  7.2 22.2 %all-to-all-start.1 = ((bf16[8,256,128]{2,1,0:T(8,128)(2,1)}), bf16[8,256,128]{2,1,0:T(8,128)(2,1)S(1)}, u32[]{:S(2)}, u32[]{:S(2)}) async-start(bf16[8,256,128]{2,1,0:T(8,128)(2,1)} %get-tuple-element.18), calls=%async_computation.1 | async-start | bytes 1048576 | tf_op jit(solution)/shard_map/all_to_all | solution.py:440
  14.5 6.2 %collective-permute-start = (bf16[8,8,256]{2,1,0:T(8,128)(2,1)}, bf16[8,8,256]{2,1,0:T(8,128)(2,1)S(1)}, u32[]{:S(2)}, u32[]{:S(2)}) collective-permute-start(bf16[8,8,256]{2,1,0:T(8,128)(2,1)} %get-tuple-element.15.own_ref), channel_id=1, source_target_pairs={{0,1},{1,2},{2,3},{3,4},{4,5},{5,6},{6,7},{8,9},{9,10},{10,11},{11... | collective-permute-start | bytes 98312 | tf_op jit(solution)/shard_map/ppermute | solution.py:426
  20.7 0.6 copy-start.3
  29.4 30.5 %copy-start.1 = (bf16[8,256,128]{2,1,0:T(8,128)(2,1)}, bf16[8,256,128]{2,1,0:T(8,128)(2,1)S(1)}, u32[]{:S(2)}) copy-start(bf16[8,256,128]{2,1,0:T(8,128)(2,1)S(1)} %all-to-all-done.1.filt_ref) | copy-start | bytes 1572868
  56.4 17.6 %all-to-all-start.3 = ((bf16[8,256,128]{2,1,0:T(8,128)(2,1)}), bf16[8,256,128]{2,1,0:T(8,128)(2,1)S(1)}, u32[]{:S(2)}, u32[]{:S(2)}) async-start(bf16[8,256,128]{2,1,0:T(8,128)(2,1)} %get-tuple-element.20), calls=%async_computation.3 | async-start | bytes 1048576 | tf_op jit(solution)/shard_map/all_to_all | solution.py:440
  74.0 4.2 %copy-start.2 = (bf16[8,256,128]{2,1,0:T(8,128)(2,1)}, bf16[8,256,128]{2,1,0:T(8,128)(2,1)S(1)}, u32[]{:S(2)}) copy-start(bf16[8,256,128]{2,1,0:T(8,128)(2,1)S(1)} %all-to-all-done.3.grad_ref) | copy-start | bytes 1572868
  74.0 23.9 %all-to-all-start.2 = ((bf16[8,272,128]{2,1,0:T(8,128)(2,1)}), bf16[8,272,128]{2,1,0:T(8,128)(2,1)}, u32[]{:S(2)}, u32[]{:S(2)}) async-start(bf16[8,272,128]{2,1,0:T(8,128)(2,1)} %get-tuple-element.19), calls=%async_computation.2 | async-start | bytes 1114112 | tf_op jit(solution)/shard_map/all_to_all | solution.py:440
  85.0 5.5 %collective-permute-start.3 = (bf16[8,64,128]{2,1,0:T(8,128)(2,1)S(1)}, bf16[8,64,128]{2,1,0:T(8,128)(2,1)S(1)}, u32[]{:S(2)}, u32[]{:S(2)}) collective-permute-start(bf16[8,64,128]{2,1,0:T(8,128)(2,1)S(1)} %get-tuple-element.29), channel_id=1, source_target_pairs={{0,16},{8,24},{16,0},{24,8},{1,17},{9,25},{17,1},{25,9},{2,18},{10... | collective-permute-start | bytes 393224 | tf_op jit(solution)/shard_map/ppermute | solution.py:453
  86.5 5.3 %collective-permute-start.4 = (bf16[8,64,128]{2,1,0:T(8,128)(2,1)S(1)}, bf16[8,64,128]{2,1,0:T(8,128)(2,1)S(1)}, u32[]{:S(2)}, u32[]{:S(2)}) collective-permute-start(bf16[8,64,128]{2,1,0:T(8,128)(2,1)S(1)} %get-tuple-element.28), channel_id=1, source_target_pairs={{0,24},{8,0},{16,8},{24,16},{1,25},{9,1},{17,9},{25,17},{2,26},{10... | collective-permute-start | bytes 393224 | tf_op jit(solution)/shard_map/ppermute | solution.py:453
  86.5 5.8 %collective-permute-start.2 = (bf16[8,64,128]{2,1,0:T(8,128)(2,1)S(1)}, bf16[8,64,128]{2,1,0:T(8,128)(2,1)S(1)}, u32[]{:S(2)}, u32[]{:S(2)}) collective-permute-start(bf16[8,64,128]{2,1,0:T(8,128)(2,1)S(1)} %get-tuple-element.27), channel_id=1, source_target_pairs={{0,8},{8,16},{16,24},{24,0},{1,9},{9,17},{17,25},{25,1},{2,10},{10... | collective-permute-start | bytes 393224 | tf_op jit(solution)/shard_map/ppermute | solution.py:453
  93.1 10.7 %copy-start.7 = (bf16[8,8,256]{2,1,0:T(8,128)(2,1)S(1)}, bf16[8,8,256]{2,1,0:T(8,128)(2,1)}, u32[]{:S(2)}) copy-start(bf16[8,8,256]{2,1,0:T(8,128)(2,1)} %get-tuple-element.16) | copy-start | bytes 98308
  93.1 12.0 %copy-start = (f32[3,2048,3]{2,1,0:T(8,128)S(1)}, f32[3,2048,3]{2,1,0:T(8,128)}, u32[]{:S(2)}) copy-start(f32[3,2048,3]{2,1,0:T(8,128)} %copy.13) | copy-start | bytes 221188
  97.9 24.8 %all-to-all-start.4 = ((bf16[8,336,128]{2,1,0:T(8,128)(2,1)}), bf16[8,336,128]{2,1,0:T(8,128)(2,1)}, u32[]{:S(2)}, u32[]{:S(2)}) async-start(bf16[8,336,128]{2,1,0:T(8,128)(2,1)} %corr.1), calls=%async_computation.4 | async-start | bytes 1376256 | tf_op jit(solution)/shard_map/all_to_all | solution.py:440
  103.8 2.8 %copy-start.6 = (f32[2048]{0:T(1024)S(1)}, f32[2048]{0:T(1024)}, u32[]{:S(2)}) copy-start(f32[2048]{0:T(1024)} %param.10) | copy-start | bytes 24580
  103.8 7.2 %collective-permute-start.1 = (bf16[8,8,256]{2,1,0:T(8,128)(2,1)S(1)}, bf16[8,8,256]{2,1,0:T(8,128)(2,1)S(1)}, u32[]{:S(2)}, u32[]{:S(2)}) collective-permute-start(bf16[8,8,256]{2,1,0:T(8,128)(2,1)S(1)} %copy-done.7), channel_id=1, source_target_pairs={{1,0},{2,1},{3,2},{4,3},{5,4},{6,5},{7,6},{9,8},{10,9},{11,10},{12... | collective-permute-start | bytes 98312 | tf_op jit(solution)/shard_map/ppermute | solution.py:427
  111.0 11.7 %copy-start.5 = (bf16[8,8,256]{2,1,0:T(8,128)(2,1)}, bf16[8,8,256]{2,1,0:T(8,128)(2,1)S(1)}, u32[]{:S(2)}) copy-start(bf16[8,8,256]{2,1,0:T(8,128)(2,1)S(1)} %collective-permute-done.1.next_ref) | copy-start | bytes 98308

commit v2 on v1

--- a/solution.py
+++ b/solution.py
@@ -8,6 +8,7 @@
 from jax.experimental import pallas as pl
 from jax.experimental.pallas import tpu as pltpu
 from jax.sharding import PartitionSpec as P
+
 
 exact_mode = lax.Precision.HIGHEST
 f32 = jnp.float32
@@ -88,10 +89,6 @@
     return (left[0] * right[0] + left[1] * right[1], left[0] * right[1] - left[1] * right[0])
 
 
-def whole(shape):
-    return pl.BlockSpec(shape, lambda k: (0,) * len(shape))
-
-
 def cost(flops, nbytes):
     return pl.CostEstimate(flops=int(flops), bytes_accessed=int(nbytes), transcendentals=0)
 
@@ -147,7 +144,7 @@
     return act
 
 
-def gate_kernel(rows, inner, proj_ref, cot_ref, prev_ref, taps_ref, gate_ref, grad_ref):
+def block_gate_kernel(rows, inner, proj_ref, cot_ref, prev_ref, taps_ref, gate_ref, grad_ref):
     taps = [flat(taps_ref[m], rows) for m in range(3)]
     first, second, value = activations(rows, inner, proj_ref, prev_ref[0], taps)
     gate_ref[0] = (first * value).astype(bf16)
@@ -218,56 +215,6 @@
 def blocks_of(quarters, inner):
     per = quarters[0].shape[1] // inner
     return [part[:, i * inner : (i + 1) * inner] for part in quarters for i in range(per)]
-
-
-def store_result(out_ref, blocks, rows, inner):
-    lanes = -(-rows // 128) * 128
-    rounded = [b.astype(bf16) for b in blocks]
-    for k, block in enumerate(rounded):
-        out_ref[k, :rows] = block
-        if k + 1 < len(rounded):
-            after = rounded[k + 1]
-            if lanes > rows:
-                after = jnp.concatenate([after, jnp.zeros((lanes - rows, inner), bf16)], axis=0)
-            tail = nt(pick(8, inner, [(0, 0), (1, 1)]), after)
-        else:
-            tail = jnp.zeros((8, lanes), f32)
-        parts = [tail[:, i : i + 128] for i in range(0, lanes, 128)]
-        out_ref[k, rows : rows + 8 * len(parts)] = jnp.concatenate(parts, axis=0).astype(bf16)
-
-
-def filter_kernel(filt_ref, small_ref, large_ref, spec_ref):
-    spectrum(filt_ref, small_ref, large_ref, spec_ref)
-
-
-def conv_kernel(gate_ref, filt_spec, small_ref, large_ref, gate_spec, out_ref):
-    n, rows, inner = gate_ref.shape
-    spectrum(gate_ref, small_ref, large_ref, gate_spec)
-    parts = product_inverse(filt_spec, gate_spec, False, small_ref, large_ref, n * inner // 4)
-    store_result(out_ref, blocks_of(parts, inner), rows, inner)
-
-
-def fgrad_kernel(grad_ref, gate_spec, small_ref, large_ref, grad_spec, out_ref):
-    n, rows, inner = grad_ref.shape
-    spectrum(grad_ref, small_ref, large_ref, grad_spec)
-    parts = product_inverse(gate_spec, grad_spec, True, small_ref, large_ref, n * inner // 4)
-    groups, _, slab, _ = out_ref.shape
-    for k, block in enumerate(blocks_of(parts, inner)):
-        for d in range(groups):
-            out_ref[d, k] = block[d * slab : (d + 1) * slab].astype(out_ref.dtype)
-
-
-def corr_kernel(grad_spec, filt_spec, small_ref, large_ref, own_ref, got_ref, out_ref):
-    n, slab, inner = own_ref.shape
-    rows = grad_spec.shape[0]
-    parts = product_inverse(filt_spec, grad_spec, True, small_ref, large_ref, n * inner // 4)
-    store_result(out_ref, blocks_of(parts, inner), rows, inner)
-    at = out_ref.shape[1] - slab
-    for k in range(n):
-        total = own_ref[k].astype(f32)
-        for e in range(got_ref.shape[0]):
-            total = total + got_ref[e, k].astype(f32)
-        out_ref[k, at:] = total.astype(bf16)
 
 
 def result_kernel(
@@ -377,7 +324,7 @@
     return (np.stack(small).astype(jnp.bfloat16), np.stack(large).astype(jnp.bfloat16))
 
 
-def shards(projections, short_filter, long_filter, skip_gain, cotangent):
+def wide_shards(projections, short_filter, long_filter, skip_gain, cotangent):
     groups = lax.axis_size("dp")
     n = lax.axis_size("ctx")
     channels = projections.shape[2]
@@ -385,7 +332,6 @@
     slab = channels // (groups * n)
     rows = groups * slab
     length = inner * n
-    q = length // 4
     tail_rows = 8 * -(-rows // 128)
 
     proj = projections.reshape(3, groups, n, slab, inner)
@@ -427,7 +373,7 @@
     after = lax.ppermute(first, "ctx", [(b, a) for a, b in forth])
 
     gate, grad = pl.pallas_call(
-        functools.partial(gate_kernel, rows, inner),
+        functools.partial(block_gate_kernel, rows, inner),
         grid=(n,),
         in_specs=[proj_spec, cot_spec, edge_spec, taps_spec],
         out_specs=[block_spec(rows), block_spec(rows)],
@@ -453,69 +399,25 @@
             got.append(lax.ppermute(piece, "dp", [(i, (i + e) % groups) for i in range(groups)]))
         return lax.dynamic_index_in_dim(pieces, me, 0, keepdims=False), jnp.stack(got)
 
-    if n % 4 == 0 and 2 * (14 * q * q) <= TABLE_BYTES:
-        small, large = (jnp.asarray(t) for t in dft_tables(q))
-        spec_shape = jax.ShapeDtypeStruct((rows, 8 * q), f32)
-        dft = 2 * rows * 14 * q * q
-
-        def call(kernel, outs, factor, name, *args):
-            return pl.pallas_call(
-                kernel,
-                out_shape=outs,
-                cost_estimate=cost(factor * dft, 30 * rows * q * 4),
-                name=name,
-            )(*args)
-
-        filt_spec = call(filter_kernel, spec_shape, 2, "filter_spectrum", filt_ch, small, large)
-        gate_spec, conv_send = call(
-            conv_kernel, [spec_shape, block_shape(rows + tail_rows)], 3, "conv", gate_ch, filt_spec, small, large
-        )
-        conv_pos = across(conv_send)
-        grad_spec, pieces = call(
-            fgrad_kernel,
-            [spec_shape, jax.ShapeDtypeStruct((groups, n, slab, inner), bf16)],
-            3,
-            "filter_gradient",
-            grad_ch,
-            gate_spec,
-            small,
-            large,
-        )
-        own, got = from_others(pieces)
-        corr_send = call(
-            corr_kernel,
-            block_shape(rows + tail_rows + slab),
-            1,
-            "corr",
-            grad_spec,
-            filt_spec,
-            small,
-            large,
-            own,
-            got,
-        )
-        corr_pos = across(corr_send)
-    else:
-
-        def grouped(value):
-            return jnp.transpose(value.reshape(n, groups, slab, inner), (1, 0, 2, 3)).astype(f32)
-
-        filt_spec = forward_dft(grouped(filt_ch))
-        gate_spec = forward_dft(grouped(gate_ch))
-        grad_spec = forward_dft(grouped(grad_ch))
-
-        def returned(spec):
-            value = jnp.transpose(inverse_dft(spec), (1, 0, 2, 3)).reshape(n, rows, inner).astype(bf16)
-            tail = jnp.transpose(value[1:, :, 0:2], (0, 2, 1))
-            lanes = 16 * tail_rows
-            tail = jnp.pad(tail, ((0, 1), (0, 6), (0, lanes - rows)))
-            tail = jnp.transpose(tail.reshape(n, 8, lanes // 128, 128), (0, 2, 1, 3)).reshape(n, tail_rows, 128)
-            return jnp.concatenate([value, tail], axis=1)
-
-        own, got = from_others(inverse_dft(conj_product(gate_spec, grad_spec)).astype(bf16))
-        total = (own.astype(f32) + jnp.sum(got.astype(f32), axis=0)).astype(bf16)
-        conv_pos = across(returned(spec_product(filt_spec, gate_spec)))
-        corr_pos = across(jnp.concatenate([returned(conj_product(filt_spec, grad_spec)), total], axis=1))
+    def grouped(value):
+        return jnp.transpose(value.reshape(n, groups, slab, inner), (1, 0, 2, 3)).astype(f32)
+
+    filt_spec = forward_dft(grouped(filt_ch))
+    gate_spec = forward_dft(grouped(gate_ch))
+    grad_spec = forward_dft(grouped(grad_ch))
+
+    def returned(spec):
+        value = jnp.transpose(inverse_dft(spec), (1, 0, 2, 3)).reshape(n, rows, inner).astype(bf16)
+        tail = jnp.transpose(value[1:, :, 0:2], (0, 2, 1))
+        lanes = 16 * tail_rows
+        tail = jnp.pad(tail, ((0, 1), (0, 6), (0, lanes - rows)))
+        tail = jnp.transpose(tail.reshape(n, 8, lanes // 128, 128), (0, 2, 1, 3)).reshape(n, tail_rows, 128)
+        return jnp.concatenate([value, tail], axis=1)
+
+    own, got = from_others(inverse_dft(conj_product(gate_spec, grad_spec)).astype(bf16))
+    total = (own.astype(f32) + jnp.sum(got.astype(f32), axis=0)).astype(bf16)
+    conv_pos = across(returned(spec_product(filt_spec, gate_spec)))
+    corr_pos = across(jnp.concatenate([returned(conj_product(filt_spec, grad_spec)), total], axis=1))
 
     layer_out, proj_grad, filter_grad = pl.pallas_call(
         functools.partial(result_kernel, rows, inner, scale),
@@ -548,6 +450,470 @@
     )
 
 
+PARTS = 3
+WIDTH = 16
+
+
+def thirds(value):
+    high = value.astype(bf16)
+    rest = value - high.astype(f32)
+    mid = rest.astype(bf16)
+    low = (rest - mid.astype(f32)).astype(bf16)
+    return [high, mid, low]
+
+
+def halves(value):
+    high = value.astype(bf16)
+    return [high, (value - high.astype(f32)).astype(bf16)]
+
+
+def spread_table(inner, count):
+    row = np.arange(PARTS * WIDTH)[:, None] % WIDTH
+    col = np.arange(count * inner)[None, :] // inner
+    return (row == col).astype(jnp.bfloat16)
+
+
+def shift_table(inner, step):
+    return np.concatenate([np.eye(inner, k=step), np.eye(inner, k=2 * step)], axis=1).astype(jnp.bfloat16)
+
+
+def spot_table(rows, cols, pairs):
+    table = np.zeros((rows, cols), np.float32)
+    for a, b in pairs:
+        table[a, b] = 1.0
+    return table.astype(jnp.bfloat16)
+
+
+def edge_table(inner):
+    return np.stack(
+        [
+            spot_table(
+                16,
+                inner,
+                ([(2 * m, inner - 2), (2 * m + 1, inner - 1)] if m < 3 else []) + [(8 + 2 * m, 0), (9 + 2 * m, 1)],
+            )
+            for m in range(4)
+        ]
+    )
+
+
+def before_table(inner):
+    return np.stack(
+        [spot_table(inner, 2 * inner, [(2 * m + 1, 0), (2 * m, inner), (2 * m + 1, inner + 1)]) for m in range(3)]
+    )
+
+
+def after_table(inner):
+    spots = []
+    for m in range(3):
+        for part in (0, 8):
+            spots += [(part + 2 * m, inner * (m + 1) - 2), (part + 2 * m + 1, inner * (m + 1) - 1)]
+    return spot_table(16, 3 * inner, spots)
+
+
+def ring(index, shift, count):
+    return lax.rem(index + shift + count, count)
+
+
+def folded(value):
+    return jnp.concatenate([value[:, i : i + 128] for i in range(0, value.shape[1], 128)], axis=0)
+
+
+def unfolded(value, rows):
+    count = value.shape[0] // rows
+    return jnp.concatenate([value[i * rows : (i + 1) * rows] for i in range(count)], axis=1)
+
+
+def param_kernel(groups, taps_ref, skip_ref, row_ref, part_ref, line_ref):
+    n, _, rows = row_ref.shape
+    slab = rows // groups
+    line_ref[...] = jnp.zeros(line_ref.shape, f32)
+    for m in range(3):
+        line_ref[3 * m : 3 * m + 3] = taps_ref[m]
+    line_ref[9:10] = skip_ref[...]
+    value = line_ref[...]
+    for k in range(n):
+        pieces = [value[:, (d * n + k) * slab : (d * n + k + 1) * slab] for d in range(groups)]
+        mine = jnp.concatenate(pieces, axis=1)
+        row_ref[k] = mine
+        part_ref[k] = jnp.concatenate(thirds(mine), axis=0)
+
+
+def send_kernel(n, me_ref, proj_ref, cot_ref, param_ref, spread_ref, shift_ref, pick_ref, *refs):
+    outs, (last_ref, first_ref, tap_ref, move_ref, stage_ref) = refs[:n], refs[n:]
+    groups, _, slab, inner = cot_ref.shape
+    rows = groups * slab
+    me = me_ref[0]
+
+    @pl.loop(0, n)
+    def _(e):
+        k = ring(me, e, n)
+        tap_ref[...] = tn(param_ref[k], spread_ref[...])
+        edges = jnp.zeros((16, rows), f32)
+        for m in range(4):
+            block = (proj_ref[m, :, k] if m < 3 else cot_ref[:, k]).reshape(rows, inner)
+            edges += nt(pick_ref[m], block)
+            if m < 3:
+                move_ref[m] = jnp.dot(block, shift_ref[...], preferred_element_type=f32)
+        last_ref[k] = edges[:8].astype(bf16)
+        first_ref[k] = edges[8:].astype(bf16)
+        stage_ref[e, 2 * rows :] = folded(edges).astype(bf16)
+        for d in range(groups):
+            here = slice(d * slab, (d + 1) * slab)
+            taps = [tap_ref[here, j * inner : (j + 1) * inner] for j in range(9)]
+            act = []
+            for m in range(3):
+                x = proj_ref[m, d, k].astype(f32)
+                x1, x2 = move_ref[m, here, :inner], move_ref[m, here, inner:]
+                act.append(taps[3 * m] * x + taps[3 * m + 1] * x1 + taps[3 * m + 2] * x2)
+            stage_ref[e, here] = (act[0] * act[2]).astype(bf16)
+            stage_ref[e, rows + d * slab : rows + (d + 1) * slab] = (cot_ref[d, k].astype(f32) * act[1]).astype(bf16)
+
+    for e in range(n):
+        outs[e][...] = stage_ref[e]
+
+
+def act_kernel(n, proj_ref, prev_ref, param_ref, spread_ref, place_ref, shift_ref, before_ref, *refs):
+    act_ref, tap_ref, move_ref = refs[-3:]
+    _, groups, _, slab, inner = proj_ref.shape
+    rows = groups * slab
+
+    @pl.loop(0, n)
+    def _(k):
+        tap_ref[...] = tn(param_ref[k], spread_ref[...])
+        early = tn(prev_ref[k], place_ref[...]).astype(bf16)
+        for m in range(3):
+            block = proj_ref[m, :, k].reshape(rows, inner)
+            both = jnp.concatenate([block, early], axis=1)
+            table = jnp.concatenate([shift_ref[...], before_ref[m]], axis=0)
+            move_ref[m] = jnp.dot(both, table, preferred_element_type=f32)
+        for d in range(groups):
+            here = slice(d * slab, (d + 1) * slab)
+            taps = [tap_ref[here, j * inner : (j + 1) * inner] for j in range(9)]
+            for m in range(3):
+                x = proj_ref[m, d, k].astype(f32)
+                x1, x2 = move_ref[m, here, :inner], move_ref[m, here, inner:]
+                act_ref[m, d, k] = taps[3 * m] * x + taps[3 * m + 1] * x1 + taps[3 * m + 2] * x2
+
+
+def pair_after(param, late, early, cot):
+    results = []
+    for t in range(2):
+        ahead = []
+        for m in range(3):
+            now = late[2 * m + t : 2 * m + t + 1]
+            one = early[2 * m + 1 : 2 * m + 2] if t == 0 else late[2 * m : 2 * m + 1]
+            two = early[2 * m : 2 * m + 1] if t == 0 else early[2 * m + 1 : 2 * m + 2]
+            taps = [param[3 * m + j : 3 * m + j + 1] for j in range(3)]
+            ahead.append(taps[0] * now + taps[1] * one + taps[2] * two)
+        gate = (ahead[0] * ahead[2]).astype(bf16)
+        grad = (cot[t : t + 1] * ahead[1]).astype(bf16)
+        results.append((ahead, gate.astype(f32), grad.astype(f32)))
+    return results
+
+
+def stacked(rows, parts):
+    line = lax.broadcasted_iota(jnp.int32, (8, rows), 0)
+    total = jnp.zeros((8, rows), f32)
+    for i, part in enumerate(parts):
+        total = jnp.where(line == i, part, total)
+    return total
+
+
+def signal_kernel(n, groups, me_ref, row_ref, fix_ref, small_ref, large_ref, *refs):
+    got = refs[:n]
+    gate_spec, grad_spec, own_ref, *pieces = refs[-groups - 6 : -4]
+    edge_ref, gate_ref, grad_ref, part_ref = refs[-4:]
+    _, rows, inner = gate_ref.shape
+    slab = rows // groups
+    me, my_group = me_ref[0], me_ref[1]
+    edge_ref[0] = jnp.zeros(edge_ref.shape[1:], f32)
+    for e in range(n):
+        edge_ref[ring(me, -e, n) + 1] = unfolded(got[e][2 * rows :].astype(f32), 16)
+    param = row_ref[me]
+    lane = lax.broadcasted_iota(jnp.int32, (rows, inner), 1)
+    for e in range(n):
+        p = ring(me, -e, n)
+        early, late = edge_ref[p], edge_ref[p + 1]
+        pair = pair_after(param, late[8:14], early[:8], late[14:16])
+        fix = stacked(rows, [pair[0][1], pair[1][1], pair[0][2], pair[1][2]])
+        placed = tn(fix.astype(bf16), fix_ref[...])
+        gate_ref[p] = jnp.where(lane < 2, placed[:, :inner], got[e][:rows].astype(f32)).astype(bf16)
+        grad_ref[p] = jnp.where(lane < 2, placed[:, inner:], got[e][rows : 2 * rows].astype(f32)).astype(bf16)
+    spectrum(gate_ref, small_ref, large_ref, gate_spec)
+    spectrum(grad_ref, small_ref, large_ref, grad_spec)
+    parts = product_inverse(gate_spec, grad_spec, True, small_ref, large_ref, n * inner // 4)
+    for k, block in enumerate(blocks_of(parts, inner)):
+        part_ref[k] = block
+    for k in range(n):
+        own_ref[k] = part_ref[k, pl.ds(pl.multiple_of(my_group * slab, slab), slab)]
+        for e in range(1, groups):
+            at = pl.multiple_of(ring(my_group, e, groups) * slab, slab)
+            pieces[e - 1][k] = part_ref[k, pl.ds(at, slab)].astype(bf16)
+
+
+def filter_kernel(groups, me_ref, small_ref, large_ref, *refs):
+    got, (spec_ref, filt_ref) = refs[:groups], refs[groups:]
+    n, slab, _ = got[0].shape
+    for e in range(groups):
+        at = pl.multiple_of(ring(me_ref[1], -e, groups) * slab, slab)
+        for k in range(n):
+            filt_ref[k, pl.ds(at, slab)] = got[e][k]
+    spectrum(filt_ref, small_ref, large_ref, spec_ref)
+
+
+def store_result(out_ref, blocks, rows, inner):
+    rounded = [b.astype(bf16) for b in blocks]
+    for k, block in enumerate(rounded):
+        out_ref[k, :rows] = block
+        if k + 1 < len(rounded):
+            tail = nt(pick(8, inner, [(0, 0), (1, 1)]), rounded[k + 1])
+        else:
+            tail = jnp.zeros((8, rows), f32)
+        out_ref[k, rows:] = folded(tail).astype(bf16)
+
+
+def conv_kernel(n, inner, filt_spec, gate_spec, small_ref, large_ref, out_ref):
+    rows = gate_spec.shape[0]
+    parts = product_inverse(filt_spec, gate_spec, False, small_ref, large_ref, n * inner // 4)
+    store_result(out_ref, blocks_of(parts, inner), rows, inner)
+
+
+def corr_kernel(n, groups, me_ref, filt_spec, grad_spec, small_ref, large_ref, conv_ref, own_ref, *refs):
+    got, outs, corr_ref = refs[: groups - 1], refs[groups - 1 : groups - 1 + n], refs[-1]
+    rows = grad_spec.shape[0]
+    height, inner = corr_ref.shape[1:]
+    parts = product_inverse(filt_spec, grad_spec, True, small_ref, large_ref, n * inner // 4)
+    store_result(corr_ref, blocks_of(parts, inner), rows, inner)
+    for e in range(n):
+        k = ring(me_ref[0], e, n)
+        outs[e][:height] = conv_ref[k]
+        outs[e][height : 2 * height] = corr_ref[k]
+        total = own_ref[k]
+        for other in got:
+            total = total + other[k].astype(f32)
+        outs[e][2 * height :] = total.astype(bf16)
+
+
+def final_kernel(
+    n, scale, me_ref, act_ref, cot_ref, last_ref, next_ref, param_ref, row_ref, spread_ref, shift_ref, after_ref, *refs
+):
+    got = refs[:n]
+    out_ref, pg_ref, fg_ref, tap_ref, late_ref, move_ref, grad_ref, stage_ref = refs[n:]
+    groups, _, slab, inner = cot_ref.shape
+    rows = groups * slab
+    height = rows + rows // 16
+    for e in range(n):
+        stage_ref[e] = got[e][...]
+
+    @pl.loop(0, n)
+    def _(e):
+        k = ring(me_ref[0], -e, n)
+        fg_ref[k] = stage_ref[e, 2 * height :].astype(f32) * scale
+        tap_ref[...] = tn(param_ref[k], spread_ref[...])
+        conv_tail = unfolded(stage_ref[e, rows:height].astype(f32), 8)
+        corr_tail = unfolded(stage_ref[e, height + rows : 2 * height].astype(f32), 8)
+        param = row_ref[k]
+        keep = param[9:10]
+        own, late = last_ref[k].astype(f32), next_ref[k].astype(f32)
+        spare = []
+        for t, (ahead, gate_t, grad_t) in enumerate(pair_after(param, late[:6], own, late[6:8])):
+            mixed_t = conv_tail[t : t + 1] + keep * gate_t
+            gate_grad_t = corr_tail[t : t + 1] + keep * grad_t
+            spare.append((gate_grad_t * ahead[2], late[6 + t : 7 + t] * mixed_t, gate_grad_t * ahead[0]))
+        ends = []
+        for m in range(3):
+            one, two = param[3 * m + 1 : 3 * m + 2], param[3 * m + 2 : 3 * m + 3]
+            ends += [two * spare[0][m], one * spare[0][m] + two * spare[1][m]]
+        late_ref[...] = tn(jnp.concatenate(halves(stacked(rows, ends)), axis=0), after_ref[...])
+        for d in range(groups):
+            here = slice(d * slab, (d + 1) * slab)
+            skip = tap_ref[here, 9 * inner : 10 * inner]
+            first, second, value = act_ref[0, d, k], act_ref[1, d, k], act_ref[2, d, k]
+            upstream = cot_ref[d, k].astype(f32)
+            gate = (first * value).astype(bf16).astype(f32)
+            grad = (upstream * second).astype(bf16).astype(f32)
+            mixed = stage_ref[e, here].astype(f32) + skip * gate
+            out_ref[d, k] = (second * mixed).astype(bf16)
+            gate_grad = stage_ref[e, height + d * slab : height + (d + 1) * slab].astype(f32) + skip * grad
+            for m, x in enumerate((gate_grad * value, upstream * mixed, gate_grad * first)):
+                high, low = halves(x)
+                move_ref[m, here, :inner] = high
+                move_ref[m, here, inner:] = low
+                grad_ref[m, here] = x
+        for m in range(3):
+            moved = jnp.dot(
+                move_ref[m], jnp.concatenate([shift_ref[...]] * 2, axis=0), preferred_element_type=f32
+            )
+            taps = [tap_ref[:, j * inner : (j + 1) * inner] for j in range(3 * m, 3 * m + 3)]
+            back = taps[0] * grad_ref[m] + taps[1] * moved[:, :inner] + taps[2] * moved[:, inner:]
+            back = (back + late_ref[:, inner * m : inner * (m + 1)]).astype(bf16)
+            for d in range(groups):
+                pg_ref[m, d, k] = back[d * slab : (d + 1) * slab]
+
+
+def peer_shards(projections, short_filter, long_filter, skip_gain, cotangent):
+    groups = lax.axis_size("dp")
+    n = lax.axis_size("ctx")
+    channels = projections.shape[2]
+    inner = projections.shape[3]
+    slab = channels // (groups * n)
+    rows = groups * slab
+    length = inner * n
+    q = length // 4
+    scale = 1.0 / math.sqrt(groups * length)
+    size = channels * inner
+
+    place = jnp.stack([lax.axis_index("ctx"), lax.axis_index("dp")]).astype(jnp.int32)
+    proj = projections.reshape(3, groups, n, slab, inner)
+    cot = cotangent.reshape(groups, n, slab, inner)
+    filt = long_filter.reshape(groups, n, slab, inner)
+    small, large = (jnp.asarray(t) for t in dft_tables(q))
+
+    def call(kernel, outs, work, args, scratch=(), limit=24):
+        moved = sum(math.prod(a.shape) * a.dtype.itemsize for a in [*args, *outs])
+
+        def full(a):
+            if a is small or a is large or (a.dtype == f32 and math.prod(a.shape) >= rows * 8 * q):
+                return pl.BlockSpec(memory_space=pltpu.VMEM)
+            return pl.BlockSpec(a.shape, lambda i, *_: (0,) * len(a.shape))
+
+        scalars = 1 if args[0] is place else 0
+        return pl.pallas_call(
+            kernel,
+            grid_spec=pltpu.PrefetchScalarGridSpec(
+                num_scalar_prefetch=scalars,
+                grid=(1,),
+                in_specs=[full(a) for a in args[scalars:]],
+                out_specs=[full(a) for a in outs],
+                scratch_shapes=list(scratch),
+            ),
+            out_shape=outs,
+            cost_estimate=cost(work, moved),
+            compiler_params=pltpu.CompilerParams(vmem_limit_bytes=limit * 2**20),
+        )(*args)
+
+    def array(*shape, dtype=bf16):
+        return jax.ShapeDtypeStruct(shape, dtype)
+
+    def to_peers(messages, axis):
+        count = lax.axis_size(axis)
+        got = []
+        for e, message in enumerate(messages, 1):
+            got.append(lax.ppermute(message, axis, [(i, (i + e) % count) for i in range(count)]))
+        return got
+
+    row_param, param = call(
+        functools.partial(param_kernel, groups),
+        [array(n, WIDTH, rows, dtype=f32), array(n, PARTS * WIDTH, rows)],
+        channels * 200,
+        [jnp.transpose(short_filter, (0, 2, 1)), skip_gain.reshape(1, channels)],
+        [pltpu.VMEM((WIDTH, channels), f32)],
+    )
+    mine = lax.dynamic_index_in_dim(filt, place[1], 0, keepdims=False).astype(bf16)
+    quarter = lax.all_to_all(mine, "ctx", split_axis=0, concat_axis=0, tiled=True)
+    spread9, spread10 = jnp.asarray(spread_table(inner, 9)), jnp.asarray(spread_table(inner, 10))
+    delay, advance = jnp.asarray(shift_table(inner, 1)), jnp.asarray(shift_table(inner, -1))
+    message = array(2 * rows + rows // 8, inner)
+    *sent, last, first = call(
+        functools.partial(send_kernel, n),
+        [message] * n + [array(n, 8, rows)] * 2,
+        2000 * size,
+        [place, proj, cot, param, spread9, delay, jnp.asarray(edge_table(inner))],
+        [
+            pltpu.VMEM((rows, 9 * inner), f32),
+            pltpu.VMEM((3, rows, 2 * inner), f32),
+            pltpu.VMEM((n, *message.shape), bf16),
+        ],
+        limit=60,
+    )
+    got = [sent[0], *to_peers(sent[1:], "ctx")]
+    forth = [(i, i + 1) for i in range(n - 1)]
+    prev = lax.ppermute(last, "ctx", forth)
+    after = lax.ppermute(first, "ctx", [(b, a) for a, b in forth])
+    shared = [quarter, *to_peers([quarter] * (groups - 1), "dp")]
+
+    dft = 2 * rows * 14 * q * q
+    spec = array(rows, 8 * q, dtype=f32)
+    (filt_spec,) = call(
+        functools.partial(filter_kernel, groups),
+        [spec],
+        2 * dft,
+        [place, small, large, *shared],
+        [pltpu.VMEM((n, rows, inner), bf16)],
+    )
+    fix = jnp.asarray(spot_table(8, 2 * inner, [(0, 0), (1, 1), (2, inner), (3, inner + 1)]))
+    gate_spec, grad_spec, own, *pieces = call(
+        functools.partial(signal_kernel, n, groups),
+        [spec, spec, array(n, slab, inner, dtype=f32)] + [array(n, slab, inner)] * (groups - 1),
+        5 * dft,
+        [place, row_param, fix, small, large, *got, prev, after, filt_spec],
+        [
+            pltpu.VMEM((n + 1, 16, rows), f32),
+            pltpu.VMEM((n, rows, inner), bf16),
+            pltpu.VMEM((n, rows, inner), bf16),
+            pltpu.VMEM((n, rows, inner), f32),
+        ],
+    )
+    others = to_peers(pieces, "dp")
+    height = rows + rows // 16
+    (conv,) = call(
+        functools.partial(conv_kernel, n, inner), [array(n, height, inner)], dft, [filt_spec, gate_spec, small, large]
+    )
+    back = array(2 * height + slab, inner)
+    sent = call(
+        functools.partial(corr_kernel, n, groups),
+        [back] * n,
+        dft,
+        [place, filt_spec, grad_spec, small, large, conv, own, *others],
+        [pltpu.VMEM((n, height, inner), bf16)],
+    )
+    got = [sent[0], *to_peers(sent[1:], "ctx")]
+    (act,) = call(
+        functools.partial(act_kernel, n),
+        [array(*proj.shape, dtype=f32)],
+        1000 * size,
+        [
+            proj, prev, param, spread9, jnp.asarray(spot_table(8, inner, [(i, i) for i in range(6)])), delay,
+            jnp.asarray(before_table(inner)), sent[0],
+        ],
+        [pltpu.VMEM((rows, 9 * inner), f32), pltpu.VMEM((3, rows, 2 * inner), f32)],
+    )
+    layer_out, proj_grad, filter_grad = call(
+        functools.partial(final_kernel, n, scale),
+        [array(*cot.shape), array(*proj.shape), array(n, slab, inner, dtype=f32)],
+        2000 * size,
+        [
+            place, act, cot, last, after, param, row_param, spread10, advance, jnp.asarray(after_table(inner)), *got
+        ],
+        [
+            pltpu.VMEM((rows, 10 * inner), f32),
+            pltpu.VMEM((rows, 3 * inner), f32),
+            pltpu.VMEM((3, rows, 2 * inner), bf16),
+            pltpu.VMEM((3, rows, inner), f32),
+            pltpu.VMEM((n, *back.shape), bf16),
+        ],
+    )
+    return (
+        layer_out.reshape(1, channels, inner),
+        proj_grad.reshape(1, 3, channels, inner),
+        filter_grad.reshape(n * slab, inner),
+    )
+
+
+def fits(mesh_sizes, channels, inner):
+    n = mesh_sizes["ctx"]
+    q = inner * n // 4
+    return n % 4 == 0 and (channels // n) % 128 == 0 and 2 * (14 * q * q) <= TABLE_BYTES
+
+
+def shards(projections, short_filter, long_filter, skip_gain, cotangent):
+    sizes = {axis: lax.axis_size(axis) for axis in ("dp", "ctx")}
+    if not fits(sizes, projections.shape[2], projections.shape[3]):
+        return wide_shards(projections, short_filter, long_filter, skip_gain, cotangent)
+    return peer_shards(projections, short_filter, long_filter, skip_gain, cotangent)
+
+
 def solution(mesh):
     placed = (P("dp", None, None, "ctx"), P(), P(None, "ctx"), P(), P("dp", None, "ctx"))
     return jax.shard_map(

time: 135 us -> 109 us (0.81)
  the two profiles are of different devices: /device:TPU:0 before, /device:TPU:13 now
where the time goes in v2:
time: 109 us; the launch traced here: 108 us
  waiting for transfers between devices  42.8 us (39%)
  starting transfers between devices  30.5 us (28%)
  Pallas kernels  29 us (27%)
  local copies, waits for them, and re-layouts  4.21 us (4%)
    ppermute x20, waiting for transfers between devices, to_peers(): lax.ppermute(message, axis, [(i, (i + e) % count) for i in range(count)])  42.8 us
    pallas_call x8, Pallas kernels, call(): pl.pallas_call(kernel, grid_spec=pltpu.PrefetchScalarGridSpec(num_scalar_...  29 us
    ppermute x20, starting transfers between devices, to_peers(): lax.ppermute(message, axis, [(i, (i + e) % count) for i in range(count)])  18.7 us
    all_to_all x1, starting transfers between devices, peer_shards(): lax.all_to_all(mine, 'ctx', split_axis=0, concat_axis=0, tiled=True)  5.66 us
    ppermute x1, starting transfers between devices, peer_shards(): prev = lax.ppermute(last, 'ctx', forth)  3.99 us
    unnamed x40, local copies, waits for them, and re-layouts  3.54 us
    ppermute x1, starting transfers between devices, peer_shards(): after = lax.ppermute(first, 'ctx', [(b, a) for a, b in forth])  2.18 us
  transfers between devices with their start and end apart: 23, of which 11 were waited for; matrix products, arithmetic and copies ran while one was open for 1% of the time, Pallas kernels for 14%

profile of v2, /device:TPU:13, one launch (start us, length us, event | category | flops | bytes accessed | tf_op | source)
XLA Modules:
  0.0 108.1 jit_solution(11586086346773972088)
XLA Ops:
  0.6 0.0 copy-start
  0.6 0.0 copy-start.1
  0.7 0.0 copy-start.3
  0.7 1.2 %copy-done = f32[2048,128]{1,0:T(8,128)S(1)} copy-done((f32[2048,128]{1,0:T(8,128)S(1)}, f32[2048,128]{1,0:T(8,128)}, u32[]{:S(2)}) %copy-start) | copy-done | bytes 1048600
  1.9 0.7 fusion
  2.5 5.7 %all-to-all-start = ((bf16[8,64,128]{2,1,0:T(8,128)(2,1)}), bf16[8,64,128]{2,1,0:T(8,128)(2,1)S(1)}, u32[]{:S(2)}, u32[]{:S(2)}) async-start(bf16[8,64,128]{2,1,0:T(8,128)(2,1)} %fusion), calls=%async_computation | async-start | bytes 262144 | tf_op jit(solution)/shard_map/all_to_all | solution.py:814
  8.2 0.9 copy-done.11
  9.1 0.7 copy-done.15
  9.8 0.1 shard_map.175
  9.9 0.0 copy-start.5
  9.9 0.7 copy-done.5
  10.6 0.6 pad_add_fusion.me_ref
  11.2 7.4 %shard_map.176 = (bf16[544,128]{1,0:T(8,128)(2,1)}, bf16[544,128]{1,0:T(8,128)(2,1)}, bf16[544,128]{1,0:T(8,128)(2,1)}, bf16[544,128]{1,0:T(8,128)(2,1)}, bf16[5...) custom-call(s32[2]{0:T(128)} %pad_add_fusion.me_ref, ...), custom_call_target="tpu_custom_call" | custom-call | flops 524288000 | bytes 3665928 | tf_op jit(solution)/shard_map/pallas_call | solution.py:782
  18.7 2.2 %collective-permute-start.11 = (bf16[8,8,256]{2,1,0:T(8,128)(2,1)}, bf16[8,8,256]{2,1,0:T(8,128)(2,1)S(1)}, u32[]{:S(2)}, u32[]{:S(2)}) collective-permute-start(bf16[8,8,256]{2,1,0:T(8,128)(2,1)} %get-tuple-element.43), channel_id=1, source_target_pairs={{1,0},{2,1},{3,2},{4,3},{5,4},{6,5},{7,6},{9,8},{10,9},{11,10},{12... | collective-permute-start | bytes 98312 | tf_op jit(solution)/shard_map/ppermute | solution.py:833
  20.9 4.0 %collective-permute-start = (bf16[8,8,256]{2,1,0:T(8,128)(2,1)}, bf16[8,8,256]{2,1,0:T(8,128)(2,1)S(1)}, u32[]{:S(2)}, u32[]{:S(2)}) collective-permute-start(bf16[8,8,256]{2,1,0:T(8,128)(2,1)} %get-tuple-element.33.last_ref), channel_id=1, source_target_pairs={{0,1},{1,2},{2,3},{3,4},{4,5},{5,6},{6,7},{8,9},{9,10},{10,11},{11... | collective-permute-start | bytes 98312 | tf_op jit(solution)/shard_map/ppermute | solution.py:832
  24.9 0.3 collective-permute-start.4
  25.2 1.2 %collective-permute-start.5 = (bf16[544,128]{1,0:T(8,128)(2,1)}, bf16[544,128]{1,0:T(8,128)(2,1)S(1)}, u32[]{:S(2)}, u32[]{:S(2)}) collective-permute-start(bf16[544,128]{1,0:T(8,128)(2,1)} %get-tuple-element.37), channel_id=1, source_target_pairs={{0,2},{1,3},{2,4},{3,5},{4,6},{5,7},{6,0},{7,1},{8,10},{9,11},{10,... | collective-permute-start | bytes 417800 | tf_op jit(solution)/shard_map/ppermute | solution.py:803
  26.4 0.0 all-to-all-done.refs_0_
  26.4 2.4 %collective-permute-start.3 = (bf16[8,64,128]{2,1,0:T(8,128)(2,1)S(1)}, bf16[8,64,128]{2,1,0:T(8,128)(2,1)S(1)}, u32[]{:S(2)}, u32[]{:S(2)}) collective-permute-start(bf16[8,64,128]{2,1,0:T(8,128)(2,1)S(1)} %all-to-all-done.refs_0_), channel_id=1, source_target_pairs={{0,24},{8,0},{16,8},{24,16},{1,25},{9,1},{17,9},{25,17},{2,26},{10... | collective-permute-start | bytes 393224 | tf_op jit(solution)/shard_map/ppermute | solution.py:803
  28.8 0.0 collective-permute-done.11.refs_9_.next_ref
  28.8 1.2 %collective-permute-start.2 = (bf16[8,64,128]{2,1,0:T(8,128)(2,1)S(1)}, bf16[8,64,128]{2,1,0:T(8,128)(2,1)S(1)}, u32[]{:S(2)}, u32[]{:S(2)}) collective-permute-start(bf16[8,64,128]{2,1,0:T(8,128)(2,1)S(1)} %all-to-all-done.refs_0_), channel_id=1, source_target_pairs={{0,16},{8,24},{16,0},{24,8},{1,17},{9,25},{17,1},{25,9},{2,18},{10... | collective-permute-start | bytes 393224 | tf_op jit(solution)/shard_map/ppermute | solution.py:803
  30.0 0.5 collective-permute-start.1
  30.5 0.0 collective-permute-done.4.refs_1_
  30.5 3.3 %collective-permute-start.6 = (bf16[544,128]{1,0:T(8,128)(2,1)}, bf16[544,128]{1,0:T(8,128)(2,1)S(1)}, u32[]{:S(2)}, u32[]{:S(2)}) collective-permute-start(bf16[544,128]{1,0:T(8,128)(2,1)} %get-tuple-element.38), channel_id=1, source_target_pairs={{0,3},{1,4},{2,5},{3,6},{4,7},{5,0},{6,1},{7,2},{8,11},{9,12},{10,... | collective-permute-start | bytes 417800 | tf_op jit(solution)/shard_map/ppermute | solution.py:803
  33.7 0.0 collective-permute-done.5.refs_2_
  33.7 0.3 collective-permute-start.7
  34.0 0.0 collective-permute-done.3.refs_3_
  34.0 1.1 %collective-permute-start.8 = (bf16[544,128]{1,0:T(8,128)(2,1)}, bf16[544,128]{1,0:T(8,128)(2,1)S(1)}, u32[]{:S(2)}, u32[]{:S(2)}) collective-permute-start(bf16[544,128]{1,0:T(8,128)(2,1)} %get-tuple-element.40), channel_id=1, source_target_pairs={{0,5},{1,6},{2,7},{3,0},{4,1},{5,2},{6,3},{7,4},{8,13},{9,14},{10,... | collective-permute-start | bytes 417800 | tf_op jit(solution)/shard_map/ppermute | solution.py:803
  35.1 0.0 collective-permute-done.2.refs_2_
  35.1 1.9 %collective-permute-start.9 = (bf16[544,128]{1,0:T(8,128)(2,1)}, bf16[544,128]{1,0:T(8,128)(2,1)S(1)}, u32[]{:S(2)}, u32[]{:S(2)}) collective-permute-start(bf16[544,128]{1,0:T(8,128)(2,1)} %get-tuple-element.41), channel_id=1, source_target_pairs={{0,6},{1,7},{2,0},{3,1},{4,2},{5,3},{6,4},{7,5},{8,14},{9,15},{10,... | collective-permute-start | bytes 417800 | tf_op jit(solution)/shard_map/ppermute | solution.py:803
  37.1 0.5 collective-permute-start.10
  37.6 1.8 %shard_map.177.refs_10_.filt_spec = f32[256,2048]{1,0:T(8,128)S(1)} custom-call(s32[2]{0:T(128)S(1)} %copy-done.16, bf16[2,256,256]{2,1,0:T(8,128)(2,1)S(1)} %copy-done.3, bf16[3,512,512]{2,1,0:T(8,128)(2,1)S(1)} %copy-done.1, bf16[8,64,128]{2,1,0:T(8,128)(2,1)S(1)} %all-to-all-done.refs_0_, bf16[8,64,128]{2,1,0:T(8,128)(2,1)S(1)} %collective-permute-done.1.refs_1_, ...), custom_call_target="tpu_custom_call" | custom-call | flops 939524096 | bytes 4456456 | tf_op jit(solution)/shard_map/pallas_call | solution.py:782
  39.4 10.0 %collective-permute-done.6.refs_3_ = bf16[544,128]{1,0:T(8,128)(2,1)S(1)} collective-permute-done((bf16[544,128]{1,0:T(8,128)(2,1)}, bf16[544,128]{1,0:T(8,128)(2,1)S(1)}, u32[]{:S(2)}, u32[]{:S(2)}) %collective-permute-start.6) | collective-permute-done | bytes 139296 | tf_op jit(solution)/shard_map/ppermute | solution.py:803
  49.4 3.0 %collective-permute-done.7.refs_4_ = bf16[544,128]{1,0:T(8,128)(2,1)S(1)} collective-permute-done((bf16[544,128]{1,0:T(8,128)(2,1)}, bf16[544,128]{1,0:T(8,128)(2,1)S(1)}, u32[]{:S(2)}, u32[]{:S(2)}) %collective-permute-start.7) | collective-permute-done | bytes 139296 | tf_op jit(solution)/shard_map/ppermute | solution.py:803
  52.4 0.0 collective-permute-done.9.refs_6_
  52.4 3.7 %collective-permute-done.10.refs_7_ = bf16[544,128]{1,0:T(8,128)(2,1)S(1)} collective-permute-done((bf16[544,128]{1,0:T(8,128)(2,1)}, bf16[544,128]{1,0:T(8,128)(2,1)S(1)}, u32[]{:S(2)}, u32[]{:S(2)}) %collective-permute-start.10) | collective-permute-done | bytes 139296 | tf_op jit(solution)/shard_map/ppermute | solution.py:803
  56.0 4.3 %shard_map.178 = (f32[256,2048]{1,0:T(8,128)S(1)}, f32[256,2048]{1,0:T(8,128)S(1)}, f32[8,64,128]{2,1,0:T(8,128)S(1)}, bf16[8,64,128]{2,1,0:T(8,128)(2,1)S(1)}, ...) custom-call(s32[2]{0:T(128)S(1)} %copy-done.16, f32[8,16,256]{2,1,0:T(8,128)S(1)} %get-tuple-element.34.row_ref, ...), custom_call_target="tpu_custom_call" | custom-call | flops 2348810240 | bytes 10096648 | tf_op jit(solution)/shard_map/pallas_call | solution.py:782
  60.3 1.6 %collective-permute-start.12 = (bf16[8,64,128]{2,1,0:T(8,128)(2,1)S(1)}, bf16[8,64,128]{2,1,0:T(8,128)(2,1)S(1)}, u32[]{:S(2)}, u32[]{:S(2)}) collective-permute-start(bf16[8,64,128]{2,1,0:T(8,128)(2,1)S(1)} %get-tuple-element.47), channel_id=1, source_target_pairs={{0,8},{8,16},{16,24},{24,0},{1,9},{9,17},{17,25},{25,1},{2,10},{10... | collective-permute-start | bytes 393224 | tf_op jit(solution)/shard_map/ppermute | solution.py:803
  62.0 0.3 collective-permute-start.13
  62.2 0.2 collective-permute-start.14
  62.4 1.1 %shard_map.179.conv_ref = bf16[8,272,128]{2,1,0:T(8,128)(2,1)S(1)} custom-call(f32[256,2048]{1,0:T(8,128)S(1)} %shard_map.177.refs_10_.filt_spec, f32[256,2048]{1,0:T(8,128)S(1)} %get-tuple-element.45.gate_spec, bf16[2,256,256]{2,1,0:T(8,128)(2,1)S(1)} %copy-done.3, bf16[3,512,512]{2,1,0:T(8,128)(2,1)S(1)} %copy-done.1), custom_call_target="tpu_custom_call" | custom-call | flops 469762048 | bytes 6586368 | tf_op jit(solution)/shard_map/pallas_call | solution.py:782
  63.6 1.1 collective-permute-done.12.refs_0_
  64.6 3.5 %collective-permute-done.13.refs_1_ = bf16[8,64,128]{2,1,0:T(8,128)(2,1)S(1)} collective-permute-done((bf16[8,64,128]{2,1,0:T(8,128)(2,1)S(1)}, bf16[8,64,128]{2,1,0:T(8,128)(2,1)S(1)}, u32[]{:S(2)}, u32[]{:S(2)}) %collective-permute-start.13) | collective-permute-done | bytes 131104 | tf_op jit(solution)/shard_map/ppermute | solution.py:803
  68.1 0.7 collective-permute-done.14.refs_2_
  68.8 0.0 copy-start.9
  68.8 0.0 copy-start.17
  68.8 1.8 %shard_map.180 = (bf16[608,128]{1,0:T(8,128)(2,1)S(1)}, bf16[608,128]{1,0:T(8,128)(2,1)S(1)}, bf16[608,128]{1,0:T(8,128)(2,1)S(1)}, bf16[608,128]{1,0:T(8,128)(2...) custom-call(s32[2]{0:T(128)S(1)} %copy-done.16, ...), custom_call_target="tpu_custom_call" | custom-call | flops 469762048 | bytes 8486920 | tf_op jit(solution)/shard_map/pallas_call | solution.py:782
  70.6 0.1 collective-permute-start.15
  70.7 0.1 collective-permute-start.16
  70.7 2.0 %collective-permute-start.17 = (bf16[608,128]{1,0:T(8,128)(2,1)S(1)}, bf16[608,128]{1,0:T(8,128)(2,1)S(1)}, u32[]{:S(2)}, u32[]{:S(2)}) collective-permute-start(bf16[608,128]{1,0:T(8,128)(2,1)S(1)} %get-tuple-element.53), channel_id=1, source_target_pairs={{0,3},{1,4},{2,5},{3,6},{4,7},{5,0},{6,1},{7,2},{8,11},{9,12},{10,... | collective-permute-start | bytes 466952 | tf_op jit(solution)/shard_map/ppermute | solution.py:803
  72.8 1.4 %collective-permute-start.18 = (bf16[608,128]{1,0:T(8,128)(2,1)S(1)}, bf16[608,128]{1,0:T(8,128)(2,1)S(1)}, u32[]{:S(2)}, u32[]{:S(2)}) collective-permute-start(bf16[608,128]{1,0:T(8,128)(2,1)S(1)} %get-tuple-element.54), channel_id=1, source_target_pairs={{0,4},{1,5},{2,6},{3,7},{4,0},{5,1},{6,2},{7,3},{8,12},{9,13},{10,... | collective-permute-start | bytes 466952 | tf_op jit(solution)/shard_map/ppermute | solution.py:803
  74.2 0.3 collective-permute-start.19
  74.5 2.0 %collective-permute-done.15.refs_1_ = bf16[608,128]{1,0:T(8,128)(2,1)S(1)} collective-permute-done((bf16[608,128]{1,0:T(8,128)(2,1)S(1)}, bf16[608,128]{1,0:T(8,128)(2,1)S(1)}, u32[]{:S(2)}, u32[]{:S(2)}) %collective-permute-start.15) | collective-permute-done | bytes 155680 | tf_op jit(solution)/shard_map/ppermute | solution.py:803
  76.6 14.5 %collective-permute-done.16.refs_2_ = bf16[608,128]{1,0:T(8,128)(2,1)S(1)} collective-permute-done((bf16[608,128]{1,0:T(8,128)(2,1)S(1)}, bf16[608,128]{1,0:T(8,128)(2,1)S(1)}, u32[]{:S(2)}, u32[]{:S(2)}) %collective-permute-start.16) | collective-permute-done | bytes 155680 | tf_op jit(solution)/shard_map/ppermute | solution.py:803
  91.0 0.0 collective-permute-start.21
  91.1 0.0 copy-start.4
  91.1 0.0 copy-start.10
  91.1 0.0 copy-start.12
  91.1 0.0 copy-start.14
  91.1 5.1 %shard_map.181.act_ref = f32[3,4,8,64,128]{4,3,2,1,0:T(8,128)S(1)} custom-call(bf16[3,4,8,64,128]{4,3,2,1,0:T(8,128)(2,1)S(1)} %bitcast.14, bf16[8,8,256]{2,1,0:T(8,128)(2,1)S(1)} %collective-permute-done.refs_8_.prev_ref, bf16[8,48,256]{2,1,0:T(8,128)(2,1)S(1)} %copy-done.6, bf16[48,1152]{1,0:T(8,128)(2,1)S(1)} %copy-done.7, bf16[8,128]{1,0:T(8,128)(2,1)S(1)} %copy-done.17, ...), custom_call_target="tpu_custom_call" | custom-call | flops 262144000 | bytes 5478400 | tf_op jit(solution)/shard_map/pallas_call | solution.py:782
  96.2 1.5 %collective-permute-done.18.refs_4_ = bf16[608,128]{1,0:T(8,128)(2,1)S(1)} collective-permute-done((bf16[608,128]{1,0:T(8,128)(2,1)S(1)}, bf16[608,128]{1,0:T(8,128)(2,1)S(1)}, u32[]{:S(2)}, u32[]{:S(2)}) %collective-permute-start.18) | collective-permute-done | bytes 155680 | tf_op jit(solution)/shard_map/ppermute | solution.py:803
  97.7 1.6 %collective-permute-done.20.refs_6_ = bf16[608,128]{1,0:T(8,128)(2,1)S(1)} collective-permute-done((bf16[608,128]{1,0:T(8,128)(2,1)S(1)}, bf16[608,128]{1,0:T(8,128)(2,1)S(1)}, u32[]{:S(2)}, u32[]{:S(2)}) %collective-permute-start.20) | collective-permute-done | bytes 155680 | tf_op jit(solution)/shard_map/ppermute | solution.py:803
  99.3 1.3 %collective-permute-done.21.refs_7_ = bf16[608,128]{1,0:T(8,128)(2,1)S(1)} collective-permute-done((bf16[608,128]{1,0:T(8,128)(2,1)S(1)}, bf16[608,128]{1,0:T(8,128)(2,1)S(1)}, u32[]{:S(2)}, u32[]{:S(2)}) %collective-permute-start.21) | collective-permute-done | bytes 155680 | tf_op jit(solution)/shard_map/ppermute | solution.py:803
  100.7 7.5 %shard_map.182 = (bf16[4,8,64,128]{3,2,1,0:T(8,128)(2,1)}, bf16[3,4,8,64,128]{4,3,2,1,0:T(8,128)(2,1)}, f32[8,64,128]{2,1,0:T(8,128)}) custom-call(s32[2]{0:T(128)S(1)} %copy-done.16, f32[3,4,8,64,128]{4,3,2,1,0:T(8,128)S(1)} %shard_map.181.act_ref, bf16[4,8,64,128]{3,2,1,0:T(8,128)(2,1)S(1)} %bitcast.16, bf16[8,8,256]{2,1,0:T(8,128)(2,1)S(1)} %copy-done.13, ...), custom_call_target="tpu_custom_call" | custom-call | flops 524288000 | bytes 7868424 | tf_op jit(solution)/shard_map/pallas_call | solution.py:782
  (32 shorter events, 0.1 us)
Async XLA Ops:
  0.6 1.2 %copy-start = (f32[2048,128]{1,0:T(8,128)S(1)}, f32[2048,128]{1,0:T(8,128)}, u32[]{:S(2)}) copy-start(f32[2048,128]{1,0:T(8,128)} %param.18) | copy-start | bytes 3145732
  0.6 36.9 %copy-start.1 = (bf16[3,512,512]{2,1,0:T(8,128)(2,1)S(1)}, bf16[3,512,512]{2,1,0:T(8,128)(2,1)}, u32[]{:S(2)}) copy-start(bf16[3,512,512]{2,1,0:T(8,128)(2,1)} %constant.37.clone.large_ref) | copy-start | bytes 4718596
  0.7 36.9 %copy-start.3 = (bf16[2,256,256]{2,1,0:T(8,128)(2,1)S(1)}, bf16[2,256,256]{2,1,0:T(8,128)(2,1)}, u32[]{:S(2)}) copy-start(bf16[2,256,256]{2,1,0:T(8,128)(2,1)} %constant.36.clone.small_ref) | copy-start | bytes 786436
  2.5 23.9 %all-to-all-start = ((bf16[8,64,128]{2,1,0:T(8,128)(2,1)}), bf16[8,64,128]{2,1,0:T(8,128)(2,1)S(1)}, u32[]{:S(2)}, u32[]{:S(2)}) async-start(bf16[8,64,128]{2,1,0:T(8,128)(2,1)} %fusion), calls=%async_computation | async-start | bytes 262144 | tf_op jit(solution)/shard_map/all_to_all | solution.py:814
  8.2 0.9 copy-start.11
  9.1 0.7 copy-start.15
  9.9 0.7 copy-start.5
  11.2 26.4 %copy-start.16 = (s32[2]{0:T(128)S(1)}, s32[2]{0:T(128)}, u32[]{:S(2)}) copy-start(s32[2]{0:T(128)} %pad_add_fusion.me_ref) | copy-start | bytes 28
  18.7 10.1 %collective-permute-start.11 = (bf16[8,8,256]{2,1,0:T(8,128)(2,1)}, bf16[8,8,256]{2,1,0:T(8,128)(2,1)S(1)}, u32[]{:S(2)}, u32[]{:S(2)}) collective-permute-start(bf16[8,8,256]{2,1,0:T(8,128)(2,1)} %get-tuple-element.43), channel_id=1, source_target_pairs={{1,0},{2,1},{3,2},{4,3},{5,4},{6,5},{7,6},{9,8},{10,9},{11,10},{12... | collective-permute-start | bytes 98312 | tf_op jit(solution)/shard_map/ppermute | solution.py:833
  20.9 9.1 %collective-permute-start = (bf16[8,8,256]{2,1,0:T(8,128)(2,1)}, bf16[8,8,256]{2,1,0:T(8,128)(2,1)S(1)}, u32[]{:S(2)}, u32[]{:S(2)}) collective-permute-start(bf16[8,8,256]{2,1,0:T(8,128)(2,1)} %get-tuple-element.33.last_ref), channel_id=1, source_target_pairs={{0,1},{1,2},{2,3},{3,4},{4,5},{5,6},{6,7},{8,9},{9,10},{10,11},{11... | collective-permute-start | bytes 98312 | tf_op jit(solution)/shard_map/ppermute | solution.py:832
  24.9 5.6 %collective-permute-start.4 = (bf16[544,128]{1,0:T(8,128)(2,1)}, bf16[544,128]{1,0:T(8,128)(2,1)S(1)}, u32[]{:S(2)}, u32[]{:S(2)}) collective-permute-start(bf16[544,128]{1,0:T(8,128)(2,1)} %get-tuple-element.36), channel_id=1, source_target_pairs={{0,1},{1,2},{2,3},{3,4},{4,5},{5,6},{6,7},{7,0},{8,9},{9,10},{10,1... | collective-permute-start | bytes 417800 | tf_op jit(solution)/shard_map/ppermute | solution.py:803
  25.2 8.5 %collective-permute-start.5 = (bf16[544,128]{1,0:T(8,128)(2,1)}, bf16[544,128]{1,0:T(8,128)(2,1)S(1)}, u32[]{:S(2)}, u32[]{:S(2)}) collective-permute-start(bf16[544,128]{1,0:T(8,128)(2,1)} %get-tuple-element.37), channel_id=1, source_target_pairs={{0,2},{1,3},{2,4},{3,5},{4,6},{5,7},{6,0},{7,1},{8,10},{9,11},{10,... | collective-permute-start | bytes 417800 | tf_op jit(solution)/shard_map/ppermute | solution.py:803
  26.4 7.6 %collective-permute-start.3 = (bf16[8,64,128]{2,1,0:T(8,128)(2,1)S(1)}, bf16[8,64,128]{2,1,0:T(8,128)(2,1)S(1)}, u32[]{:S(2)}, u32[]{:S(2)}) collective-permute-start(bf16[8,64,128]{2,1,0:T(8,128)(2,1)S(1)} %all-to-all-done.refs_0_), channel_id=1, source_target_pairs={{0,24},{8,0},{16,8},{24,16},{1,25},{9,1},{17,9},{25,17},{2,26},{10... | collective-permute-start | bytes 393224 | tf_op jit(solution)/shard_map/ppermute | solution.py:803
  28.8 6.4 %collective-permute-start.2 = (bf16[8,64,128]{2,1,0:T(8,128)(2,1)S(1)}, bf16[8,64,128]{2,1,0:T(8,128)(2,1)S(1)}, u32[]{:S(2)}, u32[]{:S(2)}) collective-permute-start(bf16[8,64,128]{2,1,0:T(8,128)(2,1)S(1)} %all-to-all-done.refs_0_), channel_id=1, source_target_pairs={{0,16},{8,24},{16,0},{24,8},{1,17},{9,25},{17,1},{25,9},{2,18},{10... | collective-permute-start | bytes 393224 | tf_op jit(solution)/shard_map/ppermute | solution.py:803
  30.0 7.1 %collective-permute-start.1 = (bf16[8,64,128]{2,1,0:T(8,128)(2,1)S(1)}, bf16[8,64,128]{2,1,0:T(8,128)(2,1)S(1)}, u32[]{:S(2)}, u32[]{:S(2)}) collective-permute-start(bf16[8,64,128]{2,1,0:T(8,128)(2,1)S(1)} %all-to-all-done.refs_0_), channel_id=1, source_target_pairs={{0,8},{8,16},{16,24},{24,0},{1,9},{9,17},{17,25},{25,1},{2,10},{10... | collective-permute-start | bytes 393224 | tf_op jit(solution)/shard_map/ppermute | solution.py:803
  30.5 18.9 %collective-permute-start.6 = (bf16[544,128]{1,0:T(8,128)(2,1)}, bf16[544,128]{1,0:T(8,128)(2,1)S(1)}, u32[]{:S(2)}, u32[]{:S(2)}) collective-permute-start(bf16[544,128]{1,0:T(8,128)(2,1)} %get-tuple-element.38), channel_id=1, source_target_pairs={{0,3},{1,4},{2,5},{3,6},{4,7},{5,0},{6,1},{7,2},{8,11},{9,12},{10,... | collective-permute-start | bytes 417800 | tf_op jit(solution)/shard_map/ppermute | solution.py:803
  33.7 18.6 %collective-permute-start.7 = (bf16[544,128]{1,0:T(8,128)(2,1)}, bf16[544,128]{1,0:T(8,128)(2,1)S(1)}, u32[]{:S(2)}, u32[]{:S(2)}) collective-permute-start(bf16[544,128]{1,0:T(8,128)(2,1)} %get-tuple-element.39), channel_id=1, source_target_pairs={{0,4},{1,5},{2,6},{3,7},{4,0},{5,1},{6,2},{7,3},{8,12},{9,13},{10,... | collective-permute-start | bytes 417800 | tf_op jit(solution)/shard_map/ppermute | solution.py:803
  34.0 18.3 %collective-permute-start.8 = (bf16[544,128]{1,0:T(8,128)(2,1)}, bf16[544,128]{1,0:T(8,128)(2,1)S(1)}, u32[]{:S(2)}, u32[]{:S(2)}) collective-permute-start(bf16[544,128]{1,0:T(8,128)(2,1)} %get-tuple-element.40), channel_id=1, source_target_pairs={{0,5},{1,6},{2,7},{3,0},{4,1},{5,2},{6,3},{7,4},{8,13},{9,14},{10,... | collective-permute-start | bytes 417800 | tf_op jit(solution)/shard_map/ppermute | solution.py:803
  35.1 17.2 %collective-permute-start.9 = (bf16[544,128]{1,0:T(8,128)(2,1)}, bf16[544,128]{1,0:T(8,128)(2,1)S(1)}, u32[]{:S(2)}, u32[]{:S(2)}) collective-permute-start(bf16[544,128]{1,0:T(8,128)(2,1)} %get-tuple-element.41), channel_id=1, source_target_pairs={{0,6},{1,7},{2,0},{3,1},{4,2},{5,3},{6,4},{7,5},{8,14},{9,15},{10,... | collective-permute-start | bytes 417800 | tf_op jit(solution)/shard_map/ppermute | solution.py:803
  37.1 18.9 %copy-start.18 = (bf16[544,128]{1,0:T(8,128)(2,1)S(1)}, bf16[544,128]{1,0:T(8,128)(2,1)}, u32[]{:S(2)}) copy-start(bf16[544,128]{1,0:T(8,128)(2,1)} %get-tuple-element.35.refs_0_) | copy-start | bytes 417796
  37.1 18.9 %copy-start.19 = (bf16[8,256]{1,0:T(8,128)(2,1)S(1)}, bf16[8,256]{1,0:T(8,128)(2,1)}, u32[]{:S(2)}) copy-start(bf16[8,256]{1,0:T(8,128)(2,1)} %constant.43.clone.fix_ref) | copy-start | bytes 12292
  37.1 18.9 %collective-permute-start.10 = (bf16[544,128]{1,0:T(8,128)(2,1)}, bf16[544,128]{1,0:T(8,128)(2,1)S(1)}, u32[]{:S(2)}, u32[]{:S(2)}) collective-permute-start(bf16[544,128]{1,0:T(8,128)(2,1)} %get-tuple-element.42), channel_id=1, source_target_pairs={{0,7},{1,0},{2,1},{3,2},{4,3},{5,4},{6,5},{7,6},{8,15},{9,8},{10,9... | collective-permute-start | bytes 417800 | tf_op jit(solution)/shard_map/ppermute | solution.py:803
  60.3 4.3 %collective-permute-start.12 = (bf16[8,64,128]{2,1,0:T(8,128)(2,1)S(1)}, bf16[8,64,128]{2,1,0:T(8,128)(2,1)S(1)}, u32[]{:S(2)}, u32[]{:S(2)}) collective-permute-start(bf16[8,64,128]{2,1,0:T(8,128)(2,1)S(1)} %get-tuple-element.47), channel_id=1, source_target_pairs={{0,8},{8,16},{16,24},{24,0},{1,9},{9,17},{17,25},{25,1},{2,10},{10... | collective-permute-start | bytes 393224 | tf_op jit(solution)/shard_map/ppermute | solution.py:803
  62.0 6.2 %collective-permute-start.13 = (bf16[8,64,128]{2,1,0:T(8,128)(2,1)S(1)}, bf16[8,64,128]{2,1,0:T(8,128)(2,1)S(1)}, u32[]{:S(2)}, u32[]{:S(2)}) collective-permute-start(bf16[8,64,128]{2,1,0:T(8,128)(2,1)S(1)} %get-tuple-element.48), channel_id=1, source_target_pairs={{0,16},{8,24},{16,0},{24,8},{1,17},{9,25},{17,1},{25,9},{2,18},{10... | collective-permute-start | bytes 393224 | tf_op jit(solution)/shard_map/ppermute | solution.py:803
  62.2 6.6 %collective-permute-start.14 = (bf16[8,64,128]{2,1,0:T(8,128)(2,1)S(1)}, bf16[8,64,128]{2,1,0:T(8,128)(2,1)S(1)}, u32[]{:S(2)}, u32[]{:S(2)}) collective-permute-start(bf16[8,64,128]{2,1,0:T(8,128)(2,1)S(1)} %get-tuple-element.49), channel_id=1, source_target_pairs={{0,24},{8,0},{16,8},{24,16},{1,25},{9,1},{17,9},{25,17},{2,26},{10... | collective-permute-start | bytes 393224 | tf_op jit(solution)/shard_map/ppermute | solution.py:803
  68.8 22.2 %copy-start.2 = (bf16[1,3,2048,128]{3,2,1,0:T(8,128)(2,1)S(1)}, bf16[1,3,2048,128]{3,2,1,0:T(8,128)(2,1)}, u32[]{:S(2)}) copy-start(bf16[1,3,2048,128]{3,2,1,0:T(8,128)(2,1)} %param.16) | copy-start | bytes 4718596
  68.8 22.2 %copy-start.6 = (bf16[8,48,256]{2,1,0:T(8,128)(2,1)S(1)}, bf16[8,48,256]{2,1,0:T(8,128)(2,1)}, u32[]{:S(2)}) copy-start(bf16[8,48,256]{2,1,0:T(8,128)(2,1)} %copy-done.5) | copy-start | bytes 589828
  68.8 22.2 %copy-start.7 = (bf16[48,1152]{1,0:T(8,128)(2,1)S(1)}, bf16[48,1152]{1,0:T(8,128)(2,1)}, u32[]{:S(2)}) copy-start(bf16[48,1152]{1,0:T(8,128)(2,1)} %constant.38.clone.spread_ref) | copy-start | bytes 331780
  68.8 22.2 %copy-start.8 = (bf16[128,256]{1,0:T(8,128)(2,1)S(1)}, bf16[128,256]{1,0:T(8,128)(2,1)}, u32[]{:S(2)}) copy-start(bf16[128,256]{1,0:T(8,128)(2,1)} %constant.40.clone.shift_ref) | copy-start | bytes 196612
  68.8 22.2 %copy-start.9 = (bf16[3,128,256]{2,1,0:T(8,128)(2,1)S(1)}, bf16[3,128,256]{2,1,0:T(8,128)(2,1)}, u32[]{:S(2)}) copy-start(bf16[3,128,256]{2,1,0:T(8,128)(2,1)} %constant.45.clone.before_ref) | copy-start | bytes 589828
  68.8 22.2 %copy-start.17 = (bf16[8,128]{1,0:T(8,128)(2,1)S(1)}, bf16[8,128]{1,0:T(8,128)(2,1)}, u32[]{:S(2)}) copy-start(bf16[8,128]{1,0:T(8,128)(2,1)} %constant.44.clone.place_ref) | copy-start | bytes 6148
  70.6 6.0 %collective-permute-start.15 = (bf16[608,128]{1,0:T(8,128)(2,1)S(1)}, bf16[608,128]{1,0:T(8,128)(2,1)S(1)}, u32[]{:S(2)}, u32[]{:S(2)}) collective-permute-start(bf16[608,128]{1,0:T(8,128)(2,1)S(1)} %get-tuple-element.51), channel_id=1, source_target_pairs={{0,1},{1,2},{2,3},{3,4},{4,5},{5,6},{6,7},{7,0},{8,9},{9,10},{10,1... | collective-permute-start | bytes 466952 | tf_op jit(solution)/shard_map/ppermute | solution.py:803
  70.7 20.4 %collective-permute-start.16 = (bf16[608,128]{1,0:T(8,128)(2,1)S(1)}, bf16[608,128]{1,0:T(8,128)(2,1)S(1)}, u32[]{:S(2)}, u32[]{:S(2)}) collective-permute-start(bf16[608,128]{1,0:T(8,128)(2,1)S(1)} %get-tuple-element.52), channel_id=1, source_target_pairs={{0,2},{1,3},{2,4},{3,5},{4,6},{5,7},{6,0},{7,1},{8,10},{9,11},{10,... | collective-permute-start | bytes 466952 | tf_op jit(solution)/shard_map/ppermute | solution.py:803
  70.7 25.5 %collective-permute-start.17 = (bf16[608,128]{1,0:T(8,128)(2,1)S(1)}, bf16[608,128]{1,0:T(8,128)(2,1)S(1)}, u32[]{:S(2)}, u32[]{:S(2)}) collective-permute-start(bf16[608,128]{1,0:T(8,128)(2,1)S(1)} %get-tuple-element.53), channel_id=1, source_target_pairs={{0,3},{1,4},{2,5},{3,6},{4,7},{5,0},{6,1},{7,2},{8,11},{9,12},{10,... | collective-permute-start | bytes 466952 | tf_op jit(solution)/shard_map/ppermute | solution.py:803
  72.8 25.0 %collective-permute-start.18 = (bf16[608,128]{1,0:T(8,128)(2,1)S(1)}, bf16[608,128]{1,0:T(8,128)(2,1)S(1)}, u32[]{:S(2)}, u32[]{:S(2)}) collective-permute-start(bf16[608,128]{1,0:T(8,128)(2,1)S(1)} %get-tuple-element.54), channel_id=1, source_target_pairs={{0,4},{1,5},{2,6},{3,7},{4,0},{5,1},{6,2},{7,3},{8,12},{9,13},{10,... | collective-permute-start | bytes 466952 | tf_op jit(solution)/shard_map/ppermute | solution.py:803
  74.2 23.5 %collective-permute-start.19 = (bf16[608,128]{1,0:T(8,128)(2,1)S(1)}, bf16[608,128]{1,0:T(8,128)(2,1)S(1)}, u32[]{:S(2)}, u32[]{:S(2)}) collective-permute-start(bf16[608,128]{1,0:T(8,128)(2,1)S(1)} %get-tuple-element.55), channel_id=1, source_target_pairs={{0,5},{1,6},{2,7},{3,0},{4,1},{5,2},{6,3},{7,4},{8,13},{9,14},{10,... | collective-permute-start | bytes 466952 | tf_op jit(solution)/shard_map/ppermute | solution.py:803
  76.6 22.8 %collective-permute-start.20 = (bf16[608,128]{1,0:T(8,128)(2,1)S(1)}, bf16[608,128]{1,0:T(8,128)(2,1)S(1)}, u32[]{:S(2)}, u32[]{:S(2)}) collective-permute-start(bf16[608,128]{1,0:T(8,128)(2,1)S(1)} %get-tuple-element.56), channel_id=1, source_target_pairs={{0,6},{1,7},{2,0},{3,1},{4,2},{5,3},{6,4},{7,5},{8,14},{9,15},{10,... | collective-permute-start | bytes 466952 | tf_op jit(solution)/shard_map/ppermute | solution.py:803
  91.0 9.6 %collective-permute-start.21 = (bf16[608,128]{1,0:T(8,128)(2,1)S(1)}, bf16[608,128]{1,0:T(8,128)(2,1)S(1)}, u32[]{:S(2)}, u32[]{:S(2)}) collective-permute-start(bf16[608,128]{1,0:T(8,128)(2,1)S(1)} %get-tuple-element.57), channel_id=1, source_target_pairs={{0,7},{1,0},{2,1},{3,2},{4,3},{5,4},{6,5},{7,6},{8,15},{9,8},{10,9... | collective-permute-start | bytes 466952 | tf_op jit(solution)/shard_map/ppermute | solution.py:803
  91.1 9.6 %copy-start.4 = (bf16[1,2048,128]{2,1,0:T(8,128)(2,1)S(1)}, bf16[1,2048,128]{2,1,0:T(8,128)(2,1)}, u32[]{:S(2)}) copy-start(bf16[1,2048,128]{2,1,0:T(8,128)(2,1)} %param.20) | copy-start | bytes 1572868
  91.1 9.5 %copy-start.10 = (bf16[48,1280]{1,0:T(8,128)(2,1)S(1)}, bf16[48,1280]{1,0:T(8,128)(2,1)}, u32[]{:S(2)}) copy-start(bf16[48,1280]{1,0:T(8,128)(2,1)} %constant.39.clone.spread_ref) | copy-start | bytes 368644
  91.1 9.5 %copy-start.12 = (bf16[128,256]{1,0:T(8,128)(2,1)S(1)}, bf16[128,256]{1,0:T(8,128)(2,1)}, u32[]{:S(2)}) copy-start(bf16[128,256]{1,0:T(8,128)(2,1)} %constant.41.clone.shift_ref) | copy-start | bytes 196612
  91.1 9.5 %copy-start.13 = (bf16[8,8,256]{2,1,0:T(8,128)(2,1)S(1)}, bf16[8,8,256]{2,1,0:T(8,128)(2,1)}, u32[]{:S(2)}) copy-start(bf16[8,8,256]{2,1,0:T(8,128)(2,1)} %get-tuple-element.33.last_ref) | copy-start | bytes 98308
  91.1 9.5 %copy-start.14 = (bf16[16,384]{1,0:T(8,128)(2,1)S(1)}, bf16[16,384]{1,0:T(8,128)(2,1)}, u32[]{:S(2)}) copy-start(bf16[16,384]{1,0:T(8,128)(2,1)} %constant.46.clone.after_ref) | copy-start | bytes 36868
